TPU v7x, 512 devices: a whole 4x4x16 slice. The times are simulated.
512 devices in a mesh: cube: 16 (over x, z_hi, core), tile: 32 (over y, z_lo).
Axes of the slice: x: 4, y: 4, z: 16 (z_hi: 2, z_lo: 8; z = z_hi * 8 + z_lo), core: 2. Of those that a mesh axis runs over, the one named last changes fastest.
Arguments:
- leaf_fronts: float32 [8, 4096, 1, 8192], P(None, 'cube', None, 'tile'), as said below
- middle_fronts: float32 [4, 4096, 1, 8192], P(None, 'cube', None, 'tile'), as said below
- root_front: float32 [2, 4096, 1, 8192], P(None, 'cube', None, 'tile'), as said below
- leaf_scatter: int32 [4, 32, 256], replicated, may hold values from 0 to 255, each once within a row
- middle_scatter: int32 [2, 32, 256], replicated, may hold values from 0 to 255, each once within a row
- leaf_orders: int32 [4], replicated, may hold values from 4096 to 8192, as said below
- middle_orders: int32 [2], replicated, may hold values from 4096 to 8192, as said below
Outputs:
- leaf_panel: bfloat16 [8, 16, 256, 256], P(None, 'cube', 'tile')
- middle_panel: bfloat16 [4, 16, 256, 256], P(None, 'cube', 'tile')
- root_panel: bfloat16 [2, 16, 256, 256], P(None, 'cube', 'tile')
- root_schur: bfloat16 [2, 4096, 1, 8192], P(None, 'cube', None, 'tile')
Inputs may be any that keep to these rules, and one draw needn't show every extreme that they name: `leaf_fronts`: each front is symmetric and positive definite. `middle_fronts`: each front is symmetric and positive definite. `root_front`: the front is symmetric and positive definite. `leaf_orders`: some front of the level has all 8192 rows live. `middle_orders`: some front of the level has all 8192 rows live.
All inputs are finite; a program needn't handle non-finite values.
Results may differ from a plain program's by a relative error of at most 0.0052.
Values may be sent and summed in bfloat16 or wider, within the bound.
A program may use at most 64 MiB of HBM per device.

v0:
```python
import jax
import jax.numpy as jnp
from jax import lax
from jax.sharding import Mesh
from jax.sharding import PartitionSpec as P

TILE = ("tile_0", "tile_1")


def partner_2(block, axis, apart):
    count = lax.axis_size(axis)
    route = []
    for low in range(count):
        high = low | 1 << apart
        if high != low and high < count:
            route += [(low, high), (high, low)]
    return lax.ppermute(block, axis, route)


def from_root(value, axes, root):
    value = jnp.where(lax.axis_index(axes) == root, value, jnp.zeros_like(value))
    for axis in axes:
        value = lax.psum(value, axis)
    return value


def bit_list(groups):
    levels = groups.bit_length() - 1
    return list(range(levels))


def spread_corner(payload, groups):
    for which_bit in bit_list(groups):
        payload = payload + partner_2(payload, "cube", which_bit)
    return payload


def spread_columns(payload, groups):
    for which_bit in bit_list(groups):
        payload = payload + partner_2(payload, "cube", which_bit)
    return payload


def solve_strip(strip_rows, corner, row_ids, pivot_tile):
    tile_width = strip_rows.shape[1]
    lower_factor = jnp.linalg.cholesky(corner)
    flat_strip = strip_rows.reshape(-1, tile_width)
    solved = jax.scipy.linalg.solve_triangular(lower_factor, flat_strip.T, lower=True).T
    solved = solved.reshape(strip_rows.shape)
    solved = jnp.where((row_ids == pivot_tile)[:, None, None], lower_factor[None], solved)
    return solved.astype(jnp.bfloat16)


def factor_level(front_block, level_depth):
    tile_size = lax.axis_size(TILE)
    groups = lax.axis_size("cube") // 2**level_depth
    pivot_tile = 2 - level_depth
    member = lax.axis_index("cube") % groups
    column_dev = lax.axis_index(TILE)
    tile_rows, tile_width, col_tiles, _ = front_block.shape
    pivot_member = pivot_tile % groups
    pivot_row = pivot_tile // groups
    pivot_dev = pivot_tile % tile_size
    pivot_col = pivot_tile // tile_size
    row_ids = jnp.arange(tile_rows, dtype=jnp.int32) * groups + member
    local_strip = front_block[:, :, pivot_col, :]
    own_column = column_dev == pivot_dev
    corner = jnp.where((member == pivot_member) & own_column, local_strip[pivot_row], 0.0)
    corner = spread_corner(corner, groups)
    identity = jnp.eye(tile_width, dtype=jnp.float32)
    corner = jnp.where(own_column, corner, identity)
    own_rows = solve_strip(local_strip, corner, row_ids, pivot_tile)
    factor_rows = from_root(own_rows, TILE, pivot_dev)
    slice_rows = tile_width // tile_size
    panel_part = lax.dynamic_slice_in_dim(factor_rows, column_dev * slice_rows, slice_rows, 1)
    zeroed = jnp.where(
        (row_ids == pivot_tile)[:, None, None], jnp.zeros_like(factor_rows), factor_rows
    )
    col_ids = jnp.arange(col_tiles, dtype=jnp.int32) * tile_size + column_dev
    picked = jnp.take(zeroed, col_ids // groups, axis=0)
    owned_mask = col_ids % groups == member
    picked = jnp.where(owned_mask[:, None, None], picked, jnp.zeros_like(picked))
    col_factor = spread_columns(picked, groups)
    update = jnp.einsum("rik,cjk->ricj", zeroed, col_factor, preferred_element_type=jnp.float32)
    return (panel_part[:, None], front_block - update)


def permute_tiles(block, row_ids, col_ids, perm_table):
    tile_width = block.shape[1]
    slot_ids = jnp.arange(tile_width, dtype=jnp.int32)
    row_perm = jnp.take(perm_table, row_ids, axis=0)
    col_perm = jnp.take(perm_table, col_ids, axis=0)
    row_onehot = (row_perm[:, None, :] == slot_ids[None, :, None]).astype(jnp.float32)
    col_onehot = (col_perm[:, None, :] == slot_ids[None, :, None]).astype(jnp.float32)
    placed = jnp.einsum("rji,ricy->rjcy", row_onehot, block, precision=lax.Precision.HIGHEST)
    return jnp.einsum("rjcy,cly->rjcl", placed, col_onehot, precision=lax.Precision.HIGHEST)


def send_up(schur_block, level_depth, order_table, scatter_table):
    tile_size = lax.axis_size(TILE)
    groups = lax.axis_size("cube") // 2**level_depth
    pivot_tile = 2 - level_depth
    cube_index = lax.axis_index("cube")
    front_id = cube_index // groups
    member = cube_index % groups
    column_dev = lax.axis_index(TILE)
    tile_rows, tile_width, col_tiles, _ = schur_block.shape
    row_ids = jnp.arange(tile_rows, dtype=jnp.int32) * groups + member
    col_ids = jnp.arange(col_tiles, dtype=jnp.int32) * tile_size + column_dev
    offsets = jnp.arange(tile_width, dtype=jnp.int32)
    live_order = order_table[front_id]
    row_keep = (row_ids[:, None] * tile_width + offsets[None, :] < live_order) & (
        row_ids[:, None] != pivot_tile
    )
    col_keep = (col_ids[:, None] * tile_width + offsets[None, :] < live_order) & (
        col_ids[:, None] != pivot_tile
    )
    keep_both = row_keep[:, :, None, None] & col_keep[None, None, :, :]
    masked = jnp.where(keep_both, schur_block, 0.0)
    parity = front_id % 2
    which_bit = groups.bit_length() - 1
    pair_shape = (tile_rows // 2, 2, tile_width, col_tiles, tile_width)
    tile_pairs = masked.reshape(pair_shape)
    kept_half = jnp.where(parity == 0, tile_pairs[:, 0], tile_pairs[:, 1])
    sent_half = jnp.where(parity == 0, tile_pairs[:, 1], tile_pairs[:, 0])
    received = partner_2(sent_half, "cube", which_bit)
    kept_ids = (jnp.arange(tile_rows // 2, dtype=jnp.int32) * 2 + parity) * groups + member
    partner = front_id + 1 - 2 * parity
    own_part = permute_tiles(kept_half, kept_ids, col_ids, scatter_table[front_id])
    other_part = permute_tiles(received, kept_ids, col_ids, scatter_table[partner])
    return own_part + other_part


def per_device(
    leaf_fronts, middle_fronts, root_front, leaf_scatter, middle_scatter, leaf_orders, middle_orders
):
    leaf_panel, leaf_schur = factor_level(leaf_fronts, 2)
    middle_input = middle_fronts + send_up(leaf_schur, 2, leaf_orders, leaf_scatter)
    middle_panel, middle_schur = factor_level(middle_input, 1)
    root_input = root_front + send_up(middle_schur, 1, middle_orders, middle_scatter)
    root_panel, root_schur = factor_level(root_input, 0)
    return (leaf_panel, middle_panel, root_panel, root_schur.astype(jnp.bfloat16))


def solution(mesh):
    split = Mesh(mesh.devices.reshape(mesh.shape["cube"], 4, 8), ("cube", "tile_0", "tile_1"))
    placed = (
        P(None, "cube", None, TILE),
        P(None, "cube", None, TILE),
        P(None, "cube", None, TILE),
        P(),
        P(),
        P(),
        P(),
    )
    return jax.shard_map(
        per_device,
        mesh=split,
        in_specs=placed,
        out_specs=(
            P(None, "cube", TILE, None),
            P(None, "cube", TILE, None),
            P(None, "cube", TILE, None),
            P(None, "cube", None, TILE),
        ),
        check_vma=False,
    )
```

profile of v0, /device:TPU:12, one launch (start us, length us, event | category | flops | bytes accessed | tf_op | source)
XLA Modules:
  0.0 1045.2 jit_solution(14356378276181455765)
XLA Ops:
  12.2 15.7 %collective-permute-start.1 = (f32[256,256]{0,1:T(8,128)S(1)}, f32[256,256]{0,1:T(8,128)S(1)}, u32[]{:S(2)}, u32[]{:S(2)}) collective-permute-start(f32[256,256]{0,1:T(8,128)S(1)} %fusion.113), channel_id=1, source_target_pairs={{0,64},{64,0},{32,96},{96,32},{128,192},{192,128},{160,224},{224,1... | collective-permute-start | bytes 786440 | tf_op jit(solution)/shard_map/ppermute | solution.py:17
  35.0 11.7 %cholesky.172 = f32[128,128]{1,0:T(8,128)S(1)} custom-call(f32[128,128]{1,0:T(8,128)S(1)} %cholesky.270), custom_call_target="Cholesky" | custom-call | tf_op jit(solution)/shard_map/jit(cholesky)/cholesky | solution.py:46
  46.8 9.8 custom-call.25
  57.1 11.7 %cholesky.189 = f32[128,128]{1,0:T(8,128)S(1)} custom-call(f32[128,128]{1,0:T(8,128)S(1)} %convolution_subtract_fusion.5), custom_call_target="Cholesky" | custom-call | tf_op jit(solution)/shard_map/jit(cholesky)/cholesky | solution.py:46
  75.1 19.7 %custom-call.20 = f32[2,128,128]{1,2,0:T(8,128)S(1)} custom-call(f32[2,128,128]{2,1,0:T(8,128)S(1)} %get-tuple-element.23), custom_call_target="InvertDiagBlocksLowerTriangular" | custom-call | tf_op jit(solution)/shard_map/jit(_solve_triangular)/triangular_solve | solution.py:48
  100.6 78.1 %all-reduce.8.cloned.1.call-done = bf16[8,256,256]{2,1,0:T(8,128)(2,1)} async-done(((bf16[8,256,256]{2,1,0:T(8,128)(2,1)}), bf16[8,256,256]{2,1,0:T(8,128)(2,1)}) %all-reduce.8.cloned.1.call-update) | async-done | bytes 1048592 | tf_op jit(solution)/shard_map/psum | solution.py:23
  179.4 132.8 %all-reduce.10.cloned.1.call-done = bf16[8,256,256]{2,1,0:T(8,128)(2,1)} async-done(((bf16[8,256,256]{2,1,0:T(8,128)(2,1)}), bf16[8,256,256]{2,1,0:T(8,128)(2,1)}) %all-reduce.10.cloned.1.call-update) | async-done | bytes 1048592 | tf_op jit(solution)/shard_map/psum | solution.py:23
  322.7 11.3 %collective-permute-done.3 = bf16[1,256,256]{2,1,0:T(8,128)(2,1)S(1)} collective-permute-done((bf16[1,256,256]{2,1,0:T(8,128)(2,1)S(1)}, bf16[1,256,256]{2,1,0:T(8,128)(2,1)S(1)}, u32[]{:S(2)}, u32[]{:S(2)}) %collective-permute-start.3) | collective-permute-done | bytes 131104 | tf_op jit(solution)/shard_map/ppermute | solution.py:17
  345.6 19.1 %collective-permute-done.4 = f32[4,256,1,256]{3,1,0,2:T(8,128)} collective-permute-done((f32[4,256,1,256]{3,1,0,2:T(8,128)}, f32[4,256,1,256]{3,1,0,2:T(8,128)}, u32[]{:S(2)}, u32[]{:S(2)}) %collective-permute-start.4) | collective-permute-done | bytes 1048608 | tf_op jit(solution)/shard_map/ppermute | solution.py:17
  380.1 15.8 %collective-permute-done.6 = f32[256,256]{0,1:T(8,128)S(1)} collective-permute-done((f32[256,256]{0,1:T(8,128)S(1)}, f32[256,256]{0,1:T(8,128)S(1)}, u32[]{:S(2)}, u32[]{:S(2)}) %collective-permute-start.6) | collective-permute-done | bytes 262176 | tf_op jit(solution)/shard_map/ppermute | solution.py:17
  406.2 11.7 %cholesky.206 = f32[128,128]{1,0:T(8,128)S(1)} custom-call(f32[128,128]{1,0:T(8,128)S(1)} %cholesky.273), custom_call_target="Cholesky" | custom-call | tf_op jit(solution)/shard_map/jit(cholesky)/cholesky | solution.py:46
  428.3 11.7 %cholesky.223 = f32[128,128]{1,0:T(8,128)S(1)} custom-call(f32[128,128]{1,0:T(8,128)S(1)} %convolution_subtract_fusion.4), custom_call_target="Cholesky" | custom-call | tf_op jit(solution)/shard_map/jit(cholesky)/cholesky | solution.py:46
  447.2 19.7 %custom-call.21 = f32[2,128,128]{1,2,0:T(8,128)S(1)} custom-call(f32[2,128,128]{2,1,0:T(8,128)S(1)} %get-tuple-element.39), custom_call_target="InvertDiagBlocksLowerTriangular" | custom-call | tf_op jit(solution)/shard_map/jit(_solve_triangular)/triangular_solve | solution.py:48
  470.6 57.2 %all-reduce.12.cloned.1.call-done = bf16[4,256,256]{2,1,0:T(8,128)(2,1)} async-done(((bf16[4,256,256]{2,1,0:T(8,128)(2,1)}), bf16[4,256,256]{2,1,0:T(8,128)(2,1)}) %all-reduce.12.cloned.1.call-update) | async-done | bytes 524304 | tf_op jit(solution)/shard_map/psum | solution.py:23
  529.1 126.9 %all-reduce.14.cloned.1.call-done = bf16[4,256,256]{2,1,0:T(8,128)(2,1)} async-done(((bf16[4,256,256]{2,1,0:T(8,128)(2,1)}), bf16[4,256,256]{2,1,0:T(8,128)(2,1)}) %all-reduce.14.cloned.1.call-update) | async-done | bytes 524304 | tf_op jit(solution)/shard_map/psum | solution.py:23
  666.4 11.7 %collective-permute-done.9 = bf16[1,256,256]{2,1,0:T(8,128)(2,1)S(1)} collective-permute-done((bf16[1,256,256]{2,1,0:T(8,128)(2,1)S(1)}, bf16[1,256,256]{2,1,0:T(8,128)(2,1)S(1)}, u32[]{:S(2)}, u32[]{:S(2)}) %collective-permute-start.9) | collective-permute-done | bytes 131104 | tf_op jit(solution)/shard_map/ppermute | solution.py:17
  690.5 12.8 %collective-permute-done.11 = f32[2,256,1,256]{1,3,0,2:T(8,128)S(1)} collective-permute-done((f32[2,256,1,256]{1,3,0,2:T(8,128)}, f32[2,256,1,256]{1,3,0,2:T(8,128)S(1)}, u32[]{:S(2)}, u32[]{:S(2)}) %collective-permute-start.11) | collective-permute-done | bytes 524320 | tf_op jit(solution)/shard_map/ppermute | solution.py:17
  715.7 16.6 %collective-permute-done.13 = f32[256,256]{0,1:T(8,128)S(1)} collective-permute-done((f32[256,256]{0,1:T(8,128)S(1)}, f32[256,256]{0,1:T(8,128)S(1)}, u32[]{:S(2)}, u32[]{:S(2)}) %collective-permute-start.13) | collective-permute-done | bytes 262176 | tf_op jit(solution)/shard_map/ppermute | solution.py:17
  753.5 11.7 %cholesky.240 = f32[128,128]{1,0:T(8,128)S(1)} custom-call(f32[128,128]{1,0:T(8,128)S(1)} %cholesky.276), custom_call_target="Cholesky" | custom-call | tf_op jit(solution)/shard_map/jit(cholesky)/cholesky | solution.py:46
  775.6 11.7 %cholesky.257 = f32[128,128]{1,0:T(8,128)S(1)} custom-call(f32[128,128]{1,0:T(8,128)S(1)} %convolution_subtract_fusion.3), custom_call_target="Cholesky" | custom-call | tf_op jit(solution)/shard_map/jit(cholesky)/cholesky | solution.py:46
  794.4 19.7 %custom-call.22 = f32[2,128,128]{1,2,0:T(8,128)S(1)} custom-call(f32[2,128,128]{2,1,0:T(8,128)S(1)} %get-tuple-element.55), custom_call_target="InvertDiagBlocksLowerTriangular" | custom-call | tf_op jit(solution)/shard_map/jit(_solve_triangular)/triangular_solve | solution.py:48
  816.6 55.6 %all-reduce.16.cloned.1.call-done = bf16[2,256,256]{2,1,0:T(8,128)(2,1)} async-done(((bf16[2,256,256]{2,1,0:T(8,128)(2,1)}), bf16[2,256,256]{2,1,0:T(8,128)(2,1)}) %all-reduce.16.cloned.1.call-update) | async-done | bytes 262160 | tf_op jit(solution)/shard_map/psum | solution.py:23
  872.2 126.7 %all-reduce.18.cloned.1.call-done = bf16[2,256,256]{2,1,0:T(8,128)(2,1)} async-done(((bf16[2,256,256]{2,1,0:T(8,128)(2,1)}), bf16[2,256,256]{2,1,0:T(8,128)(2,1)}) %all-reduce.18.cloned.1.call-update) | async-done | bytes 262160 | tf_op jit(solution)/shard_map/psum | solution.py:23
  1008.6 12.6 %collective-permute-done.17 = bf16[1,256,256]{2,1,0:T(8,128)(2,1)S(1)} collective-permute-done((bf16[1,256,256]{2,1,0:T(8,128)(2,1)S(1)}, bf16[1,256,256]{2,1,0:T(8,128)(2,1)S(1)}, u32[]{:S(2)}, u32[]{:S(2)}) %collective-permute-start.17) | collective-permute-done | bytes 131104 | tf_op jit(solution)/shard_map/ppermute | solution.py:17
  (213 shorter events, 205.8 us)
Async XLA Ops:
  7.2 171.5 %all-reduce.8.cloned.1.call-start = ((), (), s32[]{:S(2)}) async-start(), calls=%async_computation | async-start | bytes 2097152 | tf_op jit(solution)/shard_map/psum | solution.py:23
  8.7 3.4 collective-permute-start
  12.2 22.6 %collective-permute-start.1 = (f32[256,256]{0,1:T(8,128)S(1)}, f32[256,256]{0,1:T(8,128)S(1)}, u32[]{:S(2)}, u32[]{:S(2)}) collective-permute-start(f32[256,256]{0,1:T(8,128)S(1)} %fusion.113), channel_id=1, source_target_pairs={{0,64},{64,0},{32,96},{96,32},{128,192},{192,128},{160,224},{224,1... | collective-permute-start | bytes 786440 | tf_op jit(solution)/shard_map/ppermute | solution.py:17
  100.6 211.6 %all-reduce.10.cloned.1.call-start = ((), (), s32[]{:S(2)}) async-start(), calls=%async_computation.1 | async-start | bytes 2097152 | tf_op jit(solution)/shard_map/psum | solution.py:23
  178.7 349.0 %all-reduce.12.cloned.1.call-start = ((), (), s32[]{:S(2)}) async-start(), calls=%async_computation.2 | async-start | bytes 1048576 | tf_op jit(solution)/shard_map/psum | solution.py:23
  316.8 17.1 %collective-permute-start.3 = (bf16[1,256,256]{2,1,0:T(8,128)(2,1)S(1)}, bf16[1,256,256]{2,1,0:T(8,128)(2,1)S(1)}, u32[]{:S(2)}, u32[]{:S(2)}) collective-permute-start(bf16[1,256,256]{2,1,0:T(8,128)(2,1)S(1)} %fusion.112), channel_id=1, source_target_pairs={{0,64},{64,0},{32,96},{96,32},{128,192},{192,128},{160,224},{224,1... | collective-permute-start | bytes 393224 | tf_op jit(solution)/shard_map/ppermute | solution.py:17
  337.4 27.3 %collective-permute-start.4 = (f32[4,256,1,256]{3,1,0,2:T(8,128)}, f32[4,256,1,256]{3,1,0,2:T(8,128)}, u32[]{:S(2)}, u32[]{:S(2)}) collective-permute-start(f32[4,256,1,256]{3,1,0,2:T(8,128)} %select_bitcast_fusion), channel_id=1, source_target_pairs={{0,128},{128,0},{32,160},{160,32},{64,192},{192,64},{96,224},{224,... | collective-permute-start | bytes 3145736 | tf_op jit(solution)/shard_map/ppermute | solution.py:17
  367.4 3.4 collective-permute-start.5
  370.9 24.9 %collective-permute-start.6 = (f32[256,256]{0,1:T(8,128)S(1)}, f32[256,256]{0,1:T(8,128)S(1)}, u32[]{:S(2)}, u32[]{:S(2)}) collective-permute-start(f32[256,256]{0,1:T(8,128)S(1)} %fusion.111), channel_id=1, source_target_pairs={{0,64},{64,0},{32,96},{96,32},{128,192},{192,128},{160,224},{224,1... | collective-permute-start | bytes 786440 | tf_op jit(solution)/shard_map/ppermute | solution.py:17
  395.9 10.1 collective-permute-start.7
  470.4 185.5 %all-reduce.14.cloned.1.call-start = ((), (), s32[]{:S(2)}) async-start(), calls=%async_computation.3 | async-start | bytes 1048576 | tf_op jit(solution)/shard_map/psum | solution.py:23
  527.8 344.4 %all-reduce.16.cloned.1.call-start = ((), (), s32[]{:S(2)}) async-start(), calls=%async_computation.4 | async-start | bytes 524288 | tf_op jit(solution)/shard_map/psum | solution.py:23
  660.4 17.6 %collective-permute-start.9 = (bf16[1,256,256]{2,1,0:T(8,128)(2,1)S(1)}, bf16[1,256,256]{2,1,0:T(8,128)(2,1)S(1)}, u32[]{:S(2)}, u32[]{:S(2)}) collective-permute-start(bf16[1,256,256]{2,1,0:T(8,128)(2,1)S(1)} %fusion.110), channel_id=1, source_target_pairs={{0,64},{64,0},{32,96},{96,32},{128,192},{192,128},{160,224},{224,1... | collective-permute-start | bytes 393224 | tf_op jit(solution)/shard_map/ppermute | solution.py:17
  678.1 7.3 collective-permute-start.10
  686.7 16.6 %collective-permute-start.11 = (f32[2,256,1,256]{1,3,0,2:T(8,128)}, f32[2,256,1,256]{1,3,0,2:T(8,128)S(1)}, u32[]{:S(2)}, u32[]{:S(2)}) collective-permute-start(f32[2,256,1,256]{1,3,0,2:T(8,128)} %select_bitcast_fusion.1), channel_id=1, source_target_pairs={{0,256},{256,0},{32,288},{288,32},{64,320},{320,64},{96,352},{352,... | collective-permute-start | bytes 1572872 | tf_op jit(solution)/shard_map/ppermute | solution.py:17
  704.3 3.4 collective-permute-start.12
  707.7 24.6 %collective-permute-start.13 = (f32[256,256]{0,1:T(8,128)S(1)}, f32[256,256]{0,1:T(8,128)S(1)}, u32[]{:S(2)}, u32[]{:S(2)}) collective-permute-start(f32[256,256]{0,1:T(8,128)S(1)} %fusion.109), channel_id=1, source_target_pairs={{0,64},{64,0},{32,96},{96,32},{128,192},{192,128},{160,224},{224,1... | collective-permute-start | bytes 786440 | tf_op jit(solution)/shard_map/ppermute | solution.py:17
  732.3 10.1 collective-permute-start.14
  742.5 10.8 %collective-permute-start.15 = (f32[256,256]{0,1:T(8,128)S(1)}, f32[256,256]{0,1:T(8,128)S(1)}, u32[]{:S(2)}, u32[]{:S(2)}) collective-permute-start(f32[256,256]{0,1:T(8,128)S(1)} %add.403), channel_id=1, source_target_pairs={{0,256},{256,0},{32,288},{288,32},{64,320},{320,64},{96,352},{352,... | collective-permute-start | bytes 786440 | tf_op jit(solution)/shard_map/ppermute | solution.py:17
  816.6 182.4 %all-reduce.18.cloned.1.call-start = ((), (), s32[]{:S(2)}) async-start(), calls=%async_computation.5 | async-start | bytes 524288 | tf_op jit(solution)/shard_map/psum | solution.py:23
  1000.0 3.2 collective-permute-start.16
  1003.3 17.9 %collective-permute-start.17 = (bf16[1,256,256]{2,1,0:T(8,128)(2,1)S(1)}, bf16[1,256,256]{2,1,0:T(8,128)(2,1)S(1)}, u32[]{:S(2)}, u32[]{:S(2)}) collective-permute-start(bf16[1,256,256]{2,1,0:T(8,128)(2,1)S(1)} %fusion.108), channel_id=1, source_target_pairs={{0,64},{64,0},{32,96},{96,32},{128,192},{192,128},{160,224},{224,1... | collective-permute-start | bytes 393224 | tf_op jit(solution)/shard_map/ppermute | solution.py:17
  1021.2 7.3 collective-permute-start.18
  1028.6 8.4 collective-permute-start.19
  (9 other events, 644.1 us)
Sparse Core Ops, SparseCore 0:
  100.7 77.9 all-reduce.7
  181.6 130.5 all-reduce.9
  470.6 57.1 all-reduce.11
  530.5 125.4 all-reduce.13
  816.7 55.4 all-reduce.15
  874.9 123.9 all-reduce.17
where the time goes:
time: 1050 us
  waiting for transfers between devices  721 us (69%)
  other arithmetic  175 us (17%)
  starting transfers between devices  83.3 us (8%)
  local copies, waits for them, and re-layouts  27.9 us (3%)
  between operations  19.5 us (2%)
  matrix products  18 us (2%)
    psum x6, waiting for transfers between devices, from_root(): value = lax.psum(value, axis)  577 us
    ppermute x20, waiting for transfers between devices, partner_2(): return lax.ppermute(block, axis, route)  143 us
    another operation x20, other arithmetic, solve_strip(): lower_factor = jnp.linalg.cholesky(corner)  103 us
    ppermute x20, starting transfers between devices, partner_2(): return lax.ppermute(block, axis, route)  83 us
    another operation x7, other arithmetic, solve_strip(): jax.scipy.linalg.solve_triangular(lower_factor, flat_strip.T, lower=True)  59.1 us
  transfers between devices with their start and end apart: 26, of which 26 were waited for; matrix products, arithmetic and copies ran while one was open for 2% of the time, Pallas kernels for 0%

commit v1 on v0

v1 whole, which is shorter than its diff:
```python
import jax
import jax.numpy as jnp
from jax import lax
from jax.experimental import pallas as pl
from jax.experimental.pallas import tpu as pltpu
from jax.sharding import PartitionSpec as P

MESH = pl.DeviceIdType.MESH
HIGHEST = lax.Precision.HIGHEST
F32, BF16 = jnp.float32, jnp.bfloat16
W = 256


def dot(a, b, ca, cb, precision=None):
    return lax.dot_general(
        a, b, (((ca,), (cb,)), ((), ())), precision=precision, preferred_element_type=F32
    )


def inverse_factor_128(a):
    n = a.shape[0]
    rows = lax.broadcasted_iota(jnp.int32, (n, 1), 0)
    first = lax.broadcasted_iota(jnp.int32, (8, 1), 0)
    eye = lax.broadcasted_iota(jnp.int32, (n, n), 0) == lax.broadcasted_iota(jnp.int32, (n, n), 1)

    def trip(block, ab):
        a, b = ab
        live = rows < n - 8 * block
        pivots = jnp.ones((8, 1), F32)
        for i in range(8):
            row_a, row_b = a[i : i + 1, :], b[i : i + 1, :]
            pivot = a[i : i + 1, i : i + 1]
            pivots = jnp.where(first == i, pivot, pivots)
            scale = jnp.where(live & (rows > i), a[:, i : i + 1] * (1.0 / pivot), 0.0)
            a = a - scale * row_a
            b = b - scale * row_b
        b = jnp.concatenate([b[8:], b[:8] * lax.rsqrt(pivots)], 0)
        a = pltpu.roll(jnp.concatenate([a[8:], a[:8]], 0), n - 8, 1)
        return a, b

    return lax.fori_loop(0, n // 8, trip, (a, eye.astype(F32)))[1]


def inverse_factor(source, target):
    h = W // 2
    i11 = inverse_factor_128(source[:h, :h])
    l21 = dot(source[h:, :h], i11, 1, 1, HIGHEST)
    i22 = inverse_factor_128(source[h:, h:] - dot(l21, l21, 1, 1, HIGHEST))
    i21 = -dot(i22, dot(l21, i11, 1, 0, HIGHEST), 1, 0, HIGHEST)
    target[:h, :h] = i11
    target[:h, h:] = jnp.zeros((h, h), F32)
    target[h:, :h] = i21
    target[h:, h:] = i22


def solve_panel(row_block, inverse):
    return dot(row_block, inverse, 0, 1, HIGHEST)


def place(left, block, right):
    high = block.astype(BF16)
    low = (block - high.astype(F32)).astype(BF16)
    total = None
    for part in (high, low):
        moved = dot(left, part, 1, 0).astype(BF16)
        moved = dot(moved, right, 1, 1)
        total = moved if total is None else total + moved
    return total


def kernel(
    a2, a1, a0, s2, s1, o2, o1,
    leaf_out, mid_out, root_out, schur_out,
    ta2, ta1, pa, cb, rb, li, yb, l1i, l0i, hs, pl2, pm1, acc, ts, psend, precv, msend, mrecv,
    send_sem, r_ta2, r_ta1, r_pa, r_cb, r_rb, r_li, r_yb, r_l1, r_l0, r_ps, r_ms,
):
    cube, t = lax.axis_index("cube"), lax.axis_index("tile")
    x, zh, c = cube // 4, (cube // 2) % 2, cube % 2
    y, zl = t // 8, t % 8
    g = 2 * zh + c
    mover = c == zh
    pending = []

    def dev(x_, zh_, c_, y_, zl_):
        return (x_ * 4 + zh_ * 2 + c_, y_ * 8 + zl_)

    def send(pred, src, dst, recv, target):
        index = len(pending)

        def make():
            return pltpu.make_async_remote_copy(
                src_ref=src, dst_ref=dst, send_sem=send_sem.at[index], recv_sem=recv,
                device_id=target(), device_id_type=MESH,
            )

        pending.append((pred, make))

        @pl.when(pred)
        def _():
            make().start()

    def arrive(pred, dst, recv):
        @pl.when(pred)
        def _():
            pltpu.make_async_remote_copy(
                src_ref=dst, dst_ref=dst, send_sem=send_sem.at[0], recv_sem=recv,
                device_id=(cube, t), device_id_type=MESH,
            ).wait_recv()

    always = x >= 0
    is_pd0 = (zh == 0) & (c == 0)
    is_pd1 = (zh == 0) & (c == 1) & (x % 2 == 0)
    is_pd2 = (x == 0) & (zh == 1) & (c == 0)

    send((zh == 0) & (c == 1) & (x % 2 == 1), a2.at[0], pa, r_pa, lambda: dev(x - 1, zh, c, y, zl))
    for apart in (1, 3, 2):
        xd = (x + apart) % 4
        for r in range(2):
            send(always, a2.at[4 * r + xd], ta2.at[x, r], r_ta2.at[x, r], lambda xd=xd: dev(xd, zh, c, y, zl))
    xo = (x + 2) % 4
    for r in range(2):
        send(always, a1.at[2 * r + xo // 2], ta1.at[x // 2, r], r_ta1.at[x // 2, r], lambda: dev(xo, zh, c, y, zl))
    for r in range(2):
        ta2[x, r] = a2[4 * r + x]
        ta1[x // 2, r] = a1[2 * r + x // 2]

    slot = lax.broadcasted_iota(jnp.int32, (W, W), 0)
    offset = lax.broadcasted_iota(jnp.int32, (1, W), 1)

    def mover_matrix(table, orders, front, tile, pivot):
        keep = (tile * W + offset < orders[front]) & (tile != pivot)
        hit = (table[front, pl.ds(tile, 1), :] == slot) & keep
        return jnp.where(hit, 1.0, 0.0).astype(BF16)

    row_tiles = (4 * x + g, 4 * x + g + 16)

    @pl.loop(0, 4)
    def _(l):
        for w, tile in enumerate(row_tiles + (t,)):
            pl2[l, w] = mover_matrix(s2, o2, l, tile, 0)

    @pl.loop(0, 2)
    def _(m):
        for w, tile in enumerate(row_tiles + (t,)):
            pm1[m, w] = mover_matrix(s1, o1, m, tile, 1)

    lower = lax.broadcasted_iota(jnp.int32, (W, W), 0) >= lax.broadcasted_iota(jnp.int32, (W, W), 1)

    def fan_out(who, ref, recv, root_zl, ch):
        for other in range(8):
            if other != root_zl:
                send(who & (y == 0) & (zl == root_zl), ref, ref, recv, lambda o=other: dev(x, 0, ch, 0, o))
        arrive(who & ((y != 0) | (zl != root_zl)), ref, recv)
        for other in (1, 3, 2):
            send(who & (y == 0), ref, ref, recv, lambda o=other: dev(x, 0, ch, o, zl))

    @pl.when(is_pd0 & (t == 0))
    def _():
        inverse_factor(a2.at[0], li)

    fan_out(is_pd0, li, r_li, 0, 0)

    @pl.when(is_pd0)
    def _():
        panel = solve_panel(a2[0], li[...])
        cb[x] = jnp.where(lower | (t != 0), panel, 0.0).astype(BF16)

    def column_stage(k, holder, own, known):
        arrive(mover & jnp.logical_not(own), cb.at[k], r_cb.at[k])
        send(mover & jnp.logical_not(known), cb.at[k], cb.at[k], r_cb.at[k], lambda: dev(x, zh, 1 - c, y, zl))
        for apart in (1, 3, 2):
            send(mover & holder, cb.at[k], cb.at[k], r_cb.at[k], lambda a=apart: dev((x + a) % 4, zh, c, y, zl))

    def row_stage(k):
        z0 = 4 * (x % 2) + 2 * zh
        for cc in range(2):
            for r in range(2):
                line = mover & (y == x // 2 + 2 * r)
                at = z0 + cc
                source = line & (zl == at)
                ref, recv = rb.at[k, r, cc], r_rb.at[k, r, cc]

                @pl.when(source)
                def _():
                    rb[k, r, cc] = cb[k]

                arrive(mover & jnp.logical_not(source), ref, recv)
                send(line & (zl >= at) & (zl < 7), ref, ref, recv, lambda: dev(x, zh, c, y, zl + 1))
                send(line & (zl <= at) & (zl > 0), ref, ref, recv, lambda: dev(x, zh, c, y, zl - 1))
                for apart in (1, 3, 2):
                    send(line, ref, ref, recv, lambda a=apart: dev(x, zh, c, (y + a) % 4, zl))
                send(mover & (c != cc), ref, ref, recv, lambda: dev(x, zh, 1 - c, y, zl))

    for l in range(4):
        send(is_pd0 & (x == l), cb.at[l], cb.at[l], r_cb.at[l], lambda: dev(x, 1, 1, y, zl))
    for l in range(4):
        column_stage(l, x == l, is_pd0 & (x == l), always & False)
    for l in range(4):
        arrive(jnp.logical_not(mover), cb.at[l], r_cb.at[l])

    arrive(is_pd1, pa, r_pa)

    @pl.when(is_pd1)
    def _():
        total = a1[0]
        for i in range(2):
            block = a2[0] if i == 0 else pa[...]
            left = mover_matrix(s2, o2, x + i, 1, 0)
            total = total + place(left, block, pl2[x + i, 2])
        hs[...] = total

        @pl.when(t == 1)
        def _():
            for i in range(2):
                yb[i] = dot(pl2[x + i, 2], cb[x + i], 1, 0).astype(BF16)

    fan_out(is_pd1, yb, r_yb, 1, 1)

    @pl.when(is_pd1)
    def _():
        total = hs[...]
        for i in range(2):
            mine = dot(pl2[x + i, 2], cb[x + i], 1, 0).astype(BF16)
            total = total - dot(yb[i], mine, 1, 1)
        hs[...] = total

        @pl.when(t == 1)
        def _():
            inverse_factor(hs, l1i)

    fan_out(is_pd1, l1i, r_l1, 1, 1)

    @pl.when(is_pd1)
    def _():
        panel = solve_panel(hs[...], l1i[...])
        cb[4 + x // 2] = jnp.where(lower | (t != 1), panel, 0.0).astype(BF16)

    for m in range(2):
        mine = is_pd1 & (x == 2 * m)
        send(mine, cb.at[4 + m], cb.at[4 + m], r_cb.at[4 + m], lambda: dev(x, 0, 0, y, zl))
        send(mine, cb.at[4 + m], cb.at[4 + m], r_cb.at[4 + m], lambda: dev(x, 1, 1, y, zl))

    for l in range(4):
        row_stage(l)

    for l in range(4):
        for r in range(2):
            arrive(x != l, ta2.at[l, r], r_ta2.at[l, r])
    for m in range(2):
        for r in range(2):
            arrive(x // 2 != m, ta1.at[m, r], r_ta1.at[m, r])

    for r in range(2):
        ts[0] = ta1[0, r]
        ts[1] = ta1[1, r]

        @pl.loop(0, 4)
        def _(l):
            ts[l // 2] += place(pl2[l, r], ta2[l, r], pl2[l, 2])

        acc[r] = a0[r]

        @pl.loop(0, 2)
        def _(m):
            acc[r] += place(pm1[m, r], ts[m], pm1[m, 2])

    def carried(m, w, block):
        return dot(pm1[m, w], block, 1, 0).astype(BF16)

    for l in range(4):
        for r in range(2):
            arrive(jnp.logical_not(mover), rb.at[l, r, c], r_rb.at[l, r, c])

    pick = (
        lax.broadcasted_iota(jnp.int32, (8, W), 0) + 8 * t == lax.broadcasted_iota(jnp.int32, (8, W), 1)
    )
    pick = jnp.where(pick, 1.0, 0.0).astype(BF16)

    @pl.loop(0, 4)
    def _(l):
        m = l // 2
        col = carried(m, 2, dot(pl2[l, 2], cb[l], 1, 0).astype(BF16))
        for r in range(2):
            psend[l, r] = dot(pick, rb[l, r, c], 1, 0)
            row = carried(m, r, dot(pl2[l, r], rb[l, r, c], 1, 0).astype(BF16))
            acc[r] -= dot(row, col, 1, 1)

    for apart in (1, 3, 2):
        xd = (x + apart) % 4
        send(always, psend.at[xd], precv.at[x], r_ps.at[x], lambda xd=xd: dev(xd, zh, c, y, zl))
    precv[x] = psend[x]

    for m in range(2):
        column_stage(4 + m, x == 2 * m, always & False, (zh == 0) & (x == 2 * m))
    for m in range(2):
        arrive(jnp.logical_not(mover) & jnp.logical_not(is_pd1 & (x == 2 * m)), cb.at[4 + m], r_cb.at[4 + m])
    for m in range(2):
        row_stage(4 + m)
    for m in range(2):
        for r in range(2):
            arrive(jnp.logical_not(mover), rb.at[4 + m, r, c], r_rb.at[4 + m, r, c])

    @pl.loop(0, 2)
    def _(m):
        col = carried(m, 2, cb[4 + m])
        for r in range(2):
            msend[m, r] = dot(pick, rb[4 + m, r, c], 1, 0)
            acc[r] -= dot(carried(m, r, rb[4 + m, r, c]), col, 1, 1)

    send(always, msend.at[xo // 2], mrecv.at[x // 2], r_ms.at[x // 2], lambda: dev(xo, zh, c, y, zl))
    mrecv[x // 2] = msend[x // 2]

    @pl.when(is_pd2)
    def _():
        high = acc[0].astype(BF16)
        cb[6] = high
        cb[7] = (acc[0] - high.astype(F32)).astype(BF16)

    for k in (6, 7):
        send(is_pd2, cb.at[k], cb.at[k], r_cb.at[k], lambda: dev(0, 1, 1, y, zl))
        send(is_pd2, cb.at[k], cb.at[k], r_cb.at[k], lambda: dev(0, 0, 0, y, zl))

    @pl.when(is_pd2 & (t == 2))
    def _():
        inverse_factor(acc.at[0], l0i)

    root = is_pd2 & (t == 2)
    send(root, l0i, l0i, r_l0, lambda: dev(0, 1, 1, 0, 2))

    for k in (6, 7):
        column_stage(k, x == 0, always & False, (zh == 1) & (x == 0))
    for k in (6, 7):
        row_stage(k)
    for k in (6, 7):
        arrive(jnp.logical_not(mover) & jnp.logical_not(is_pd2), cb.at[k], r_cb.at[k])
        for r in range(2):
            arrive(jnp.logical_not(mover), rb.at[k, r, c], r_rb.at[k, r, c])

    arrive(jnp.logical_not(root), l0i, r_l0)
    two = mover & (y == 0) & (zl == 2)
    send(two & (x == 0) & (zh == 1), l0i, l0i, r_l0, lambda: dev(0, 0, 0, 0, 2))
    for other in (1, 3, 2):
        send(two & (x == 0), l0i, l0i, r_l0, lambda o=other: dev(o, zh, c, 0, 2))
    for other in (1, 3, 2):
        send(two, l0i, l0i, r_l0, lambda o=other: dev(x, zh, c, o, 2))
    for other in (3, 1, 4, 0, 5, 6, 7):
        send(mover & (zl == 2), l0i, l0i, r_l0, lambda o=other: dev(x, zh, c, y, o))
    send(
        mover & jnp.logical_not((x == 0) & (zh == 1) & (t == 2)),
        l0i, l0i, r_l0, lambda: dev(x, zh, 1 - c, y, zl),
    )

    def last_panel(high, low):
        return solve_panel(high.astype(F32) + low.astype(F32), l0i[...])

    col = last_panel(cb[6], cb[7])
    col = jnp.where(t == 2, 0.0, col).astype(BF16)
    for r in range(2):
        tile = row_tiles[r]
        full = last_panel(rb[6, r, c], rb[7, r, c])
        full = jnp.where(lower | (tile != 2), full, 0.0).astype(BF16)
        root_out[r, 0] = dot(pick, full, 1, 0).astype(BF16)
        row = jnp.where(tile == 2, jnp.zeros_like(full), full)
        schur_out[r, :, 0, :] = (acc[r] - dot(row, col, 1, 1)).astype(BF16)

    for s in range(4):
        arrive(x != s, precv.at[s], r_ps.at[s])
    for s in range(2):
        arrive(x // 2 != s, mrecv.at[s], r_ms.at[s])
    for s in range(4):
        for r in range(2):
            leaf_out[4 * r + s, 0] = precv[s, r].astype(BF16)
    for s in range(2):
        for r in range(2):
            mid_out[2 * r + s, 0] = mrecv[s, r].astype(BF16)

    for pred, make in pending:

        @pl.when(pred)
        def _(make=make):
            make().wait_send()


def per_device(leaf, middle, root, s2, s1, o2, o1):
    vmem = pl.BlockSpec(memory_space=pltpu.VMEM)
    smem = pl.BlockSpec(memory_space=pltpu.SMEM)
    dma = pltpu.SemaphoreType.DMA
    outs = [
        jax.ShapeDtypeStruct((8, 1, 8, W), BF16),
        jax.ShapeDtypeStruct((4, 1, 8, W), BF16),
        jax.ShapeDtypeStruct((2, 1, 8, W), BF16),
        jax.ShapeDtypeStruct((2, W, 1, W), BF16),
    ]
    tile = (W, W)
    scratch = [
        pltpu.VMEM((4, 2) + tile, F32),
        pltpu.VMEM((2, 2) + tile, F32),
        pltpu.VMEM(tile, F32),
        pltpu.VMEM((8,) + tile, BF16),
        pltpu.VMEM((8, 2, 2) + tile, BF16),
        pltpu.VMEM(tile, F32),
        pltpu.VMEM((2,) + tile, BF16),
        pltpu.VMEM(tile, F32),
        pltpu.VMEM(tile, F32),
        pltpu.VMEM(tile, F32),
        pltpu.VMEM((4, 3) + tile, BF16),
        pltpu.VMEM((2, 3) + tile, BF16),
        pltpu.VMEM((2,) + tile, F32),
        pltpu.VMEM((2,) + tile, F32),
        pltpu.VMEM((4, 2, 8, W), F32),
        pltpu.VMEM((4, 2, 8, W), F32),
        pltpu.VMEM((2, 2, 8, W), F32),
        pltpu.VMEM((2, 2, 8, W), F32),
        dma((SENDS,)),
        dma((4, 2)), dma((2, 2)), dma, dma((8,)), dma((8, 2, 2)),
        dma, dma, dma, dma, dma((4,)), dma((2,)),
    ]
    return pl.pallas_call(
        kernel,
        out_shape=outs,
        in_specs=[vmem] * 5 + [smem] * 2,
        out_specs=[vmem] * 4,
        scratch_shapes=scratch,
        compiler_params=pltpu.CompilerParams(has_side_effects=True, vmem_limit_bytes=60 * 2**20),
        name="window",
    )(leaf.reshape(8, W, W), middle.reshape(4, W, W), root.reshape(2, W, W), s2, s1, o2, o1)


SENDS = 360


def solution(mesh):
    return jax.shard_map(
        per_device,
        mesh=mesh,
        in_specs=(P(None, "cube", None, "tile"),) * 3 + (P(),) * 4,
        out_specs=(P(None, "cube", "tile", None),) * 3 + (P(None, "cube", None, "tile"),),
        check_vma=False,
    )
```

time: 1050 us -> 433 us (0.41)
  the two profiles are of different devices: /device:TPU:12 before, /device:TPU:243 now
where the time goes in v1:
time: 433 us; the launch traced here: 432 us
  Pallas kernels  420 us (97%)
  local copies, waits for them, and re-layouts  11.6 us (3%)
    pallas_call x1, Pallas kernels, per_device(): pl.pallas_call(kernel, out_shape=outs, in_specs=[vmem] * 5 + [smem] * 2,...  420 us
    unnamed x8, local copies, waits for them, and re-layouts  9.86 us

profile of v1, /device:TPU:243, one launch (start us, length us, event | category | flops | bytes accessed | tf_op | source)
XLA Modules:
  0.0 432.2 jit_solution(17530653417866869113)
XLA Ops:
  0.6 0.0 copy-start
  0.6 2.0 copy.20
  2.7 2.3 copy.19
  4.9 0.0 copy-done
  4.9 1.6 copy.18
  6.5 419.9 %window.1 = (bf16[8,1,8,256]{3,2,1,0:T(8,128)(2,1)}, bf16[4,1,8,256]{3,2,1,0:T(8,128)(2,1)}, bf16[2,1,8,256]{3,2,1,0:T(8,128)(2,1)}, bf16[2,256,1,256]{3,2,1,0:T(2,128)(2,1)}) custom-call(f32[8,256,256]{2,1,0:T(8,128)} %bitcast.9, f32[4,256,256]{2,1,0:T(8,128)} %bitcast.10, f32[2,256,256]{2,1,0:T(8,128)} %bitcast.11, s32[4,32,256]{2,1,0:T(8,128)} %s2_.1, ...), custom_call_target="tpu_custom_call" | custom-call | tf_op jit(solution)/shard_map/window/pallas_call | solution.py:418
  426.4 1.8 copy.11
  428.2 1.4 copy.24
  429.5 1.3 copy.25
  430.9 1.3 copy.26
Async XLA Ops:
  0.6 4.3 copy-start

commit v2 on v1

--- a/solution.py
+++ b/solution.py
@@ -93,6 +93,7 @@
                 device_id=target(), device_id_type=MESH,
             )
 
+        assert index < SENDS
         pending.append((pred, make))
 
         @pl.when(pred)
@@ -146,6 +147,18 @@
 
     lower = lax.broadcasted_iota(jnp.int32, (W, W), 0) >= lax.broadcasted_iota(jnp.int32, (W, W), 1)
 
+    half = W // 2
+
+    def pieces(ref, recv):
+        return (
+            (ref.at[:half, :half], recv.at[0]),
+            (ref.at[half : half + half // 2], recv.at[1]),
+            (ref.at[half + half // 2 :], recv.at[2]),
+        )
+
+    def clear_upper(ref):
+        ref[:half, half:] = jnp.zeros((half, half), F32)
+
     def fan_out(who, ref, recv, root_zl, ch):
         for other in range(8):
             if other != root_zl:
@@ -158,7 +171,12 @@
     def _():
         inverse_factor(a2.at[0], li)
 
-    fan_out(is_pd0, li, r_li, 0, 0)
+    @pl.when(jnp.logical_not(is_pd0 & (t == 0)))
+    def _():
+        clear_upper(li)
+
+    for part, recv in pieces(li, r_li):
+        fan_out(is_pd0, part, recv, 0, 0)
 
     @pl.when(is_pd0)
     def _():
@@ -171,25 +189,31 @@
         for apart in (1, 3, 2):
             send(mover & holder, cb.at[k], cb.at[k], r_cb.at[k], lambda a=apart: dev((x + a) % 4, zh, c, y, zl))
 
+    def line(r):
+        return mover & (y == x // 2 + 2 * r)
+
     def row_stage(k):
         z0 = 4 * (x % 2) + 2 * zh
         for cc in range(2):
             for r in range(2):
-                line = mover & (y == x // 2 + 2 * r)
                 at = z0 + cc
-                source = line & (zl == at)
+                source = line(r) & (zl == at)
                 ref, recv = rb.at[k, r, cc], r_rb.at[k, r, cc]
 
                 @pl.when(source)
                 def _():
                     rb[k, r, cc] = cb[k]
 
-                arrive(mover & jnp.logical_not(source), ref, recv)
-                send(line & (zl >= at) & (zl < 7), ref, ref, recv, lambda: dev(x, zh, c, y, zl + 1))
-                send(line & (zl <= at) & (zl > 0), ref, ref, recv, lambda: dev(x, zh, c, y, zl - 1))
+                arrive(line(r) & (zl != at), ref, recv)
+                send(line(r) & (zl >= at) & (zl < 7), ref, ref, recv, lambda: dev(x, zh, c, y, zl + 1))
+                send(line(r) & (zl <= at) & (zl > 0), ref, ref, recv, lambda: dev(x, zh, c, y, zl - 1))
                 for apart in (1, 3, 2):
-                    send(line, ref, ref, recv, lambda a=apart: dev(x, zh, c, (y + a) % 4, zl))
-                send(mover & (c != cc), ref, ref, recv, lambda: dev(x, zh, 1 - c, y, zl))
+                    send(line(r), ref, ref, recv, lambda a=apart, cc=cc: dev(x, zh, cc, (y + a) % 4, zl))
+                send(line(r) & (c != cc), ref, ref, recv, lambda: dev(x, zh, 1 - c, y, zl))
+
+    def rows_here(k):
+        for r in range(2):
+            arrive(jnp.logical_not(line(r)), rb.at[k, r, c], r_rb.at[k, r, c])
 
     for l in range(4):
         send(is_pd0 & (x == l), cb.at[l], cb.at[l], r_cb.at[l], lambda: dev(x, 1, 1, y, zl))
@@ -228,7 +252,12 @@
         def _():
             inverse_factor(hs, l1i)
 
-    fan_out(is_pd1, l1i, r_l1, 1, 1)
+    @pl.when(jnp.logical_not(is_pd1 & (t == 1)))
+    def _():
+        clear_upper(l1i)
+
+    for part, recv in pieces(l1i, r_l1):
+        fan_out(is_pd1, part, recv, 1, 1)
 
     @pl.when(is_pd1)
     def _():
@@ -266,29 +295,6 @@
 
     def carried(m, w, block):
         return dot(pm1[m, w], block, 1, 0).astype(BF16)
-
-    for l in range(4):
-        for r in range(2):
-            arrive(jnp.logical_not(mover), rb.at[l, r, c], r_rb.at[l, r, c])
-
-    pick = (
-        lax.broadcasted_iota(jnp.int32, (8, W), 0) + 8 * t == lax.broadcasted_iota(jnp.int32, (8, W), 1)
-    )
-    pick = jnp.where(pick, 1.0, 0.0).astype(BF16)
-
-    @pl.loop(0, 4)
-    def _(l):
-        m = l // 2
-        col = carried(m, 2, dot(pl2[l, 2], cb[l], 1, 0).astype(BF16))
-        for r in range(2):
-            psend[l, r] = dot(pick, rb[l, r, c], 1, 0)
-            row = carried(m, r, dot(pl2[l, r], rb[l, r, c], 1, 0).astype(BF16))
-            acc[r] -= dot(row, col, 1, 1)
-
-    for apart in (1, 3, 2):
-        xd = (x + apart) % 4
-        send(always, psend.at[xd], precv.at[x], r_ps.at[x], lambda xd=xd: dev(xd, zh, c, y, zl))
-    precv[x] = psend[x]
 
     for m in range(2):
         column_stage(4 + m, x == 2 * m, always & False, (zh == 0) & (x == 2 * m))
@@ -296,9 +302,27 @@
         arrive(jnp.logical_not(mover) & jnp.logical_not(is_pd1 & (x == 2 * m)), cb.at[4 + m], r_cb.at[4 + m])
     for m in range(2):
         row_stage(4 + m)
-    for m in range(2):
-        for r in range(2):
-            arrive(jnp.logical_not(mover), rb.at[4 + m, r, c], r_rb.at[4 + m, r, c])
+    for k in range(6):
+        rows_here(k)
+
+    pick = (
+        lax.broadcasted_iota(jnp.int32, (8, W), 0) + 8 * t == lax.broadcasted_iota(jnp.int32, (8, W), 1)
+    )
+    pick = jnp.where(pick, 1.0, 0.0).astype(BF16)
+
+    @pl.loop(0, 4)
+    def _(l):
+        m = l // 2
+        col = carried(m, 2, dot(pl2[l, 2], cb[l], 1, 0).astype(BF16))
+        for r in range(2):
+            psend[l, r] = dot(pick, rb[l, r, c], 1, 0)
+            row = carried(m, r, dot(pl2[l, r], rb[l, r, c], 1, 0).astype(BF16))
+            acc[r] -= dot(row, col, 1, 1)
+
+    for apart in (1, 3, 2):
+        xd = (x + apart) % 4
+        send(always, psend.at[xd], precv.at[x], r_ps.at[x], lambda xd=xd: dev(xd, zh, c, y, zl))
+    precv[x] = psend[x]
 
     @pl.loop(0, 2)
     def _(m):
@@ -325,7 +349,13 @@
         inverse_factor(acc.at[0], l0i)
 
     root = is_pd2 & (t == 2)
-    send(root, l0i, l0i, r_l0, lambda: dev(0, 1, 1, 0, 2))
+
+    @pl.when(jnp.logical_not(root))
+    def _():
+        clear_upper(l0i)
+
+    for part, recv in pieces(l0i, r_l0):
+        send(root, part, part, recv, lambda: dev(0, 1, 1, 0, 2))
 
     for k in (6, 7):
         column_stage(k, x == 0, always & False, (zh == 1) & (x == 0))
@@ -333,22 +363,22 @@
         row_stage(k)
     for k in (6, 7):
         arrive(jnp.logical_not(mover) & jnp.logical_not(is_pd2), cb.at[k], r_cb.at[k])
-        for r in range(2):
-            arrive(jnp.logical_not(mover), rb.at[k, r, c], r_rb.at[k, r, c])
-
-    arrive(jnp.logical_not(root), l0i, r_l0)
+        rows_here(k)
+
     two = mover & (y == 0) & (zl == 2)
-    send(two & (x == 0) & (zh == 1), l0i, l0i, r_l0, lambda: dev(0, 0, 0, 0, 2))
-    for other in (1, 3, 2):
-        send(two & (x == 0), l0i, l0i, r_l0, lambda o=other: dev(o, zh, c, 0, 2))
-    for other in (1, 3, 2):
-        send(two, l0i, l0i, r_l0, lambda o=other: dev(x, zh, c, o, 2))
-    for other in (3, 1, 4, 0, 5, 6, 7):
-        send(mover & (zl == 2), l0i, l0i, r_l0, lambda o=other: dev(x, zh, c, y, o))
-    send(
-        mover & jnp.logical_not((x == 0) & (zh == 1) & (t == 2)),
-        l0i, l0i, r_l0, lambda: dev(x, zh, 1 - c, y, zl),
-    )
+    for part, recv in pieces(l0i, r_l0):
+        arrive(jnp.logical_not(root), part, recv)
+        send(two & (x == 0) & (zh == 1), part, part, recv, lambda: dev(0, 0, 0, 0, 2))
+        for other in (1, 3, 2):
+            send(two & (x == 0), part, part, recv, lambda o=other: dev(o, zh, c, 0, 2))
+        for other in (1, 3, 2):
+            send(two, part, part, recv, lambda o=other: dev(x, zh, c, o, 2))
+        for at, other in ((2, 5), (2, 3), (2, 1), (5, 7), (5, 6), (3, 4), (1, 0)):
+            send(mover & (zl == at), part, part, recv, lambda o=other: dev(x, zh, c, y, o))
+        send(
+            mover & jnp.logical_not((x == 0) & (zh == 1) & (t == 2)),
+            part, part, recv, lambda: dev(x, zh, 1 - c, y, zl),
+        )
 
     def last_panel(high, low):
         return solve_panel(high.astype(F32) + low.astype(F32), l0i[...])
@@ -413,7 +443,7 @@
         pltpu.VMEM((2, 2, 8, W), F32),
         dma((SENDS,)),
         dma((4, 2)), dma((2, 2)), dma, dma((8,)), dma((8, 2, 2)),
-        dma, dma, dma, dma, dma((4,)), dma((2,)),
+        dma((3,)), dma, dma((3,)), dma((3,)), dma((4,)), dma((2,)),
     ]
     return pl.pallas_call(
         kernel,
@@ -426,7 +456,7 @@
     )(leaf.reshape(8, W, W), middle.reshape(4, W, W), root.reshape(2, W, W), s2, s1, o2, o1)
 
 
-SENDS = 360
+SENDS = 420
 
 
 def solution(mesh):

time: 433 us -> 245 us (0.57)
  the two profiles are of different devices: /device:TPU:243 before, /device:TPU:19 now
where the time goes in v2:
time: 245 us
  Pallas kernels  232 us (95%)
  local copies, waits for them, and re-layouts  11.6 us (5%)
    pallas_call x1, Pallas kernels, per_device(): pl.pallas_call(kernel, out_shape=outs, in_specs=[vmem] * 5 + [smem] * 2,...  232 us
    unnamed x8, local copies, waits for them, and re-layouts  9.86 us

profile of v2, /device:TPU:19, one launch (start us, length us, event | category | flops | bytes accessed | tf_op | source)
XLA Modules:
  0.0 244.5 jit_solution(9176174144884763600)
XLA Ops:
  0.6 0.0 copy-start
  0.6 2.0 copy.20
  2.7 2.3 copy.19
  4.9 0.0 copy-done
  4.9 1.6 copy.18
  6.5 232.2 %window.1 = (bf16[8,1,8,256]{3,2,1,0:T(8,128)(2,1)}, bf16[4,1,8,256]{3,2,1,0:T(8,128)(2,1)}, bf16[2,1,8,256]{3,2,1,0:T(8,128)(2,1)}, bf16[2,256,1,256]{3,2,1,0:T(2,128)(2,1)}) custom-call(f32[8,256,256]{2,1,0:T(8,128)} %bitcast.9, f32[4,256,256]{2,1,0:T(8,128)} %bitcast.10, f32[2,256,256]{2,1,0:T(8,128)} %bitcast.11, s32[4,32,256]{2,1,0:T(8,128)} %s2_.1, ...), custom_call_target="tpu_custom_call" | custom-call | tf_op jit(solution)/shard_map/window/pallas_call | solution.py:448
  238.7 1.8 copy.11
  240.5 1.4 copy.24
  241.9 1.3 copy.25
  243.2 1.3 copy.26
Async XLA Ops:
  0.6 4.3 %copy-start = (f32[8,256,1,256]{3,2,1,0:T(1,128)S(1)}, f32[8,256,1,256]{3,2,1,0:T(1,128)}, u32[]{:S(2)}) copy-start(f32[8,256,1,256]{3,2,1,0:T(1,128)} %param.7) | copy-start | bytes 6291460

commit v3 on v2

--- a/solution.py
+++ b/solution.py
@@ -9,6 +9,11 @@
 HIGHEST = lax.Precision.HIGHEST
 F32, BF16 = jnp.float32, jnp.bfloat16
 W = 256
+TREES = (
+    ((0, 3), (0, 1), (3, 5), (3, 4), (1, 2), (5, 7), (5, 6)),
+    ((1, 4), (1, 2), (1, 0), (4, 6), (4, 5), (2, 3), (6, 7)),
+    ((2, 5), (2, 3), (2, 1), (5, 7), (5, 6), (3, 4), (1, 0)),
+)
 
 
 def dot(a, b, ca, cb, precision=None):
@@ -71,8 +76,8 @@
 def kernel(
     a2, a1, a0, s2, s1, o2, o1,
     leaf_out, mid_out, root_out, schur_out,
-    ta2, ta1, pa, cb, rb, li, yb, l1i, l0i, hs, pl2, pm1, acc, ts, psend, precv, msend, mrecv,
-    send_sem, r_ta2, r_ta1, r_pa, r_cb, r_rb, r_li, r_yb, r_l1, r_l0, r_ps, r_ms,
+    ta2, ta1, pa, cb, rb, li, yb, l1i, l0i, hs, pl2, pm1, acc, ts, psend, precv, msend, mrecv, rel, vb, hp,
+    send_sem, r_ta2, r_ta1, r_pa, r_cb, r_rb, r_li, r_yb, r_l1, r_l0, r_ps, r_ms, r_rel, r_vb,
 ):
     cube, t = lax.axis_index("cube"), lax.axis_index("tile")
     x, zh, c = cube // 4, (cube // 2) % 2, cube % 2
@@ -114,13 +119,29 @@
     is_pd2 = (x == 0) & (zh == 1) & (c == 0)
 
     send((zh == 0) & (c == 1) & (x % 2 == 1), a2.at[0], pa, r_pa, lambda: dev(x - 1, zh, c, y, zl))
-    for apart in (1, 3, 2):
-        xd = (x + apart) % 4
-        for r in range(2):
-            send(always, a2.at[4 * r + xd], ta2.at[x, r], r_ta2.at[x, r], lambda xd=xd: dev(xd, zh, c, y, zl))
     xo = (x + 2) % 4
-    for r in range(2):
-        send(always, a1.at[2 * r + xo // 2], ta1.at[x // 2, r], r_ta1.at[x // 2, r], lambda: dev(xo, zh, c, y, zl))
+
+    def exchange(who):
+        for step in (1, 3):
+            xd = (x + step) % 4
+            r = step // 2
+            for j, src in ((0, a2.at[4 * r + xo]), (1, a1.at[2 * r + xo // 2])):
+                send(who, src, rel.at[r, j], r_rel.at[r, j], lambda xd=xd: dev(xd, zh, c, y, zl))
+        for step in (1, 3):
+            xd = (x + step) % 4
+            for r in range(2):
+                send(who, a2.at[4 * r + xd], ta2.at[x, r], r_ta2.at[x, r], lambda xd=xd: dev(xd, zh, c, y, zl))
+
+    def pass_on(who):
+        for step in (1, 3):
+            xd, xs = (x + step) % 4, (x + 4 - step) % 4
+            r = step // 2
+            for j, dst, recv in ((0, ta2.at[xs, r], r_ta2.at[xs, r]), (1, ta1.at[xs // 2, r], r_ta1.at[xs // 2, r])):
+                arrive(who, rel.at[r, j], r_rel.at[r, j])
+                send(who, rel.at[r, j], dst, recv, lambda xd=xd: dev(xd, zh, c, y, zl))
+
+    late = t == 1
+    exchange(jnp.logical_not(late))
     for r in range(2):
         ta2[x, r] = a2[4 * r + x]
         ta1[x // 2, r] = a1[2 * r + x // 2]
@@ -160,13 +181,15 @@
         ref[:half, half:] = jnp.zeros((half, half), F32)
 
     def fan_out(who, ref, recv, root_zl, ch):
-        for other in range(8):
-            if other != root_zl:
-                send(who & (y == 0) & (zl == root_zl), ref, ref, recv, lambda o=other: dev(x, 0, ch, 0, o))
         arrive(who & ((y != 0) | (zl != root_zl)), ref, recv)
+        for at, other in TREES[root_zl]:
+            send(who & (y == 0) & (zl == at), ref, ref, recv, lambda o=other: dev(x, 0, ch, 0, o))
         for other in (1, 3, 2):
             send(who & (y == 0), ref, ref, recv, lambda o=other: dev(x, 0, ch, o, zl))
 
+    busy = is_pd0 & (t == 0)
+    pass_on(jnp.logical_not(late | busy))
+
     @pl.when(is_pd0 & (t == 0))
     def _():
         inverse_factor(a2.at[0], li)
@@ -177,6 +200,8 @@
 
     for part, recv in pieces(li, r_li):
         fan_out(is_pd0, part, recv, 0, 0)
+
+    pass_on(busy)
 
     @pl.when(is_pd0)
     def _():
@@ -219,6 +244,67 @@
         send(is_pd0 & (x == l), cb.at[l], cb.at[l], r_cb.at[l], lambda: dev(x, 1, 1, y, zl))
     for l in range(4):
         column_stage(l, x == l, is_pd0 & (x == l), always & False)
+    def root_tiles(who):
+        for l in range(4):
+            for r in range(2):
+                arrive(who & (x != l), ta2.at[l, r], r_ta2.at[l, r])
+        for m in range(2):
+            for r in range(2):
+                arrive(who & (x // 2 != m), ta1.at[m, r], r_ta1.at[m, r])
+
+        @pl.when(who)
+        def _():
+            @pl.loop(0, 2)
+            def _(r):
+                ts[0] = ta1[0, r]
+                ts[1] = ta1[1, r]
+
+                @pl.loop(0, 4)
+                def _(l):
+                    ts[l // 2] += place(pl2[l, r], ta2[l, r], pl2[l, 2])
+
+                acc[r] = a0[r]
+
+                @pl.loop(0, 2)
+                def _(m):
+                    acc[r] += place(pm1[m, r], ts[m], pm1[m, 2])
+
+    exchange(late)
+    pass_on(late & jnp.logical_not(mover))
+    early = (zh == 1) & (c == 0)
+    root_tiles(early)
+
+    @pl.when(is_pd2)
+    def _():
+        high = acc[0].astype(BF16)
+        cb[6] = high
+        cb[7] = (acc[0] - high.astype(F32)).astype(BF16)
+
+    for k in (6, 7):
+        send(is_pd2, cb.at[k], cb.at[k], r_cb.at[k], lambda: dev(0, 1, 1, y, zl))
+        send(is_pd2, cb.at[k], cb.at[k], r_cb.at[k], lambda: dev(0, 0, 0, y, zl))
+
+    def carried(m, w, block):
+        return dot(pm1[m, w], block, 1, 0).astype(BF16)
+
+    def column_of(k):
+        if k < 4:
+            return carried(k // 2, 2, dot(pl2[k, 2], cb[k], 1, 0).astype(BF16))
+        return carried(k - 4, 2, cb[k])
+
+    def pivot_stage(k):
+        @pl.when(mover & (t == 2))
+        def _():
+            vb[k] = column_of(k)
+
+        zero = mover & (y == 0)
+        arrive(zero & (zl != 2), vb.at[k], r_vb.at[k])
+        send(zero & (zl >= 2) & (zl < 7), vb.at[k], vb.at[k], r_vb.at[k], lambda: dev(x, zh, c, y, zl + 1))
+        send(zero & (zl <= 2) & (zl > 0), vb.at[k], vb.at[k], r_vb.at[k], lambda: dev(x, zh, c, y, zl - 1))
+        for other in (1, 3, 2):
+            send(zero, vb.at[k], vb.at[k], r_vb.at[k], lambda o=other: dev(x, zh, c, o, zl))
+        send(zero, vb.at[k], vb.at[k], r_vb.at[k], lambda: dev(x, zh, 1 - c, y, zl))
+
     for l in range(4):
         arrive(jnp.logical_not(mover), cb.at[l], r_cb.at[l])
 
@@ -238,7 +324,8 @@
             for i in range(2):
                 yb[i] = dot(pl2[x + i, 2], cb[x + i], 1, 0).astype(BF16)
 
-    fan_out(is_pd1, yb, r_yb, 1, 1)
+    for i in range(2):
+        fan_out(is_pd1, yb.at[i], r_yb.at[i], 1, 1)
 
     @pl.when(is_pd1)
     def _():
@@ -271,44 +358,55 @@
 
     for l in range(4):
         row_stage(l)
-
     for l in range(4):
-        for r in range(2):
-            arrive(x != l, ta2.at[l, r], r_ta2.at[l, r])
-    for m in range(2):
-        for r in range(2):
-            arrive(x // 2 != m, ta1.at[m, r], r_ta1.at[m, r])
-
-    for r in range(2):
-        ts[0] = ta1[0, r]
-        ts[1] = ta1[1, r]
-
-        @pl.loop(0, 4)
-        def _(l):
-            ts[l // 2] += place(pl2[l, r], ta2[l, r], pl2[l, 2])
-
-        acc[r] = a0[r]
-
-        @pl.loop(0, 2)
-        def _(m):
-            acc[r] += place(pm1[m, r], ts[m], pm1[m, 2])
-
-    def carried(m, w, block):
-        return dot(pm1[m, w], block, 1, 0).astype(BF16)
-
+        pivot_stage(l)
+    pass_on(late & mover)
+    root_tiles(jnp.logical_not(early))
+    for k in (6, 7):
+        column_stage(k, x == 0, always & False, (zh == 1) & (x == 0))
+    for k in (6, 7):
+        row_stage(k)
     for m in range(2):
         column_stage(4 + m, x == 2 * m, always & False, (zh == 0) & (x == 2 * m))
     for m in range(2):
         arrive(jnp.logical_not(mover) & jnp.logical_not(is_pd1 & (x == 2 * m)), cb.at[4 + m], r_cb.at[4 + m])
+
+    root = is_pd2 & (t == 2)
+
+    @pl.when(root)
+    def _():
+        total = acc[0]
+        for k in range(6):
+            block = column_of(k)
+            total = total - dot(block, block, 1, 1)
+        hs[...] = total
+        inverse_factor(hs, l0i)
+
+    @pl.when(jnp.logical_not(root))
+    def _():
+        clear_upper(l0i)
+
+    for part, recv in pieces(l0i, r_l0):
+        send(root, part, part, recv, lambda: dev(0, 1, 1, 0, 2))
+
     for m in range(2):
         row_stage(4 + m)
+    for m in range(2):
+        pivot_stage(4 + m)
     for k in range(6):
-        rows_here(k)
+        arrive(mover & (y != 0), vb.at[k], r_vb.at[k])
+        send(mover & (y != 0), vb.at[k], vb.at[k], r_vb.at[k], lambda: dev(x, zh, 1 - c, y, zl))
+    for l in range(4):
+        rows_here(l)
+    for k in range(4):
+        arrive(jnp.logical_not(mover), vb.at[k], r_vb.at[k])
 
     pick = (
         lax.broadcasted_iota(jnp.int32, (8, W), 0) + 8 * t == lax.broadcasted_iota(jnp.int32, (8, W), 1)
     )
     pick = jnp.where(pick, 1.0, 0.0).astype(BF16)
+
+    hp[...] = jnp.zeros_like(hp)
 
     @pl.loop(0, 4)
     def _(l):
@@ -318,52 +416,13 @@
             psend[l, r] = dot(pick, rb[l, r, c], 1, 0)
             row = carried(m, r, dot(pl2[l, r], rb[l, r, c], 1, 0).astype(BF16))
             acc[r] -= dot(row, col, 1, 1)
+            hp[r] -= dot(vb[l], row, 1, 1)
+        hp[2] -= dot(vb[l], col, 1, 1)
 
     for apart in (1, 3, 2):
         xd = (x + apart) % 4
         send(always, psend.at[xd], precv.at[x], r_ps.at[x], lambda xd=xd: dev(xd, zh, c, y, zl))
     precv[x] = psend[x]
-
-    @pl.loop(0, 2)
-    def _(m):
-        col = carried(m, 2, cb[4 + m])
-        for r in range(2):
-            msend[m, r] = dot(pick, rb[4 + m, r, c], 1, 0)
-            acc[r] -= dot(carried(m, r, rb[4 + m, r, c]), col, 1, 1)
-
-    send(always, msend.at[xo // 2], mrecv.at[x // 2], r_ms.at[x // 2], lambda: dev(xo, zh, c, y, zl))
-    mrecv[x // 2] = msend[x // 2]
-
-    @pl.when(is_pd2)
-    def _():
-        high = acc[0].astype(BF16)
-        cb[6] = high
-        cb[7] = (acc[0] - high.astype(F32)).astype(BF16)
-
-    for k in (6, 7):
-        send(is_pd2, cb.at[k], cb.at[k], r_cb.at[k], lambda: dev(0, 1, 1, y, zl))
-        send(is_pd2, cb.at[k], cb.at[k], r_cb.at[k], lambda: dev(0, 0, 0, y, zl))
-
-    @pl.when(is_pd2 & (t == 2))
-    def _():
-        inverse_factor(acc.at[0], l0i)
-
-    root = is_pd2 & (t == 2)
-
-    @pl.when(jnp.logical_not(root))
-    def _():
-        clear_upper(l0i)
-
-    for part, recv in pieces(l0i, r_l0):
-        send(root, part, part, recv, lambda: dev(0, 1, 1, 0, 2))
-
-    for k in (6, 7):
-        column_stage(k, x == 0, always & False, (zh == 1) & (x == 0))
-    for k in (6, 7):
-        row_stage(k)
-    for k in (6, 7):
-        arrive(jnp.logical_not(mover) & jnp.logical_not(is_pd2), cb.at[k], r_cb.at[k])
-        rows_here(k)
 
     two = mover & (y == 0) & (zl == 2)
     for part, recv in pieces(l0i, r_l0):
@@ -373,21 +432,42 @@
             send(two & (x == 0), part, part, recv, lambda o=other: dev(o, zh, c, 0, 2))
         for other in (1, 3, 2):
             send(two, part, part, recv, lambda o=other: dev(x, zh, c, o, 2))
-        for at, other in ((2, 5), (2, 3), (2, 1), (5, 7), (5, 6), (3, 4), (1, 0)):
+        for at, other in TREES[2]:
             send(mover & (zl == at), part, part, recv, lambda o=other: dev(x, zh, c, y, o))
         send(
             mover & jnp.logical_not((x == 0) & (zh == 1) & (t == 2)),
             part, part, recv, lambda: dev(x, zh, 1 - c, y, zl),
         )
 
-    def last_panel(high, low):
-        return solve_panel(high.astype(F32) + low.astype(F32), l0i[...])
-
-    col = last_panel(cb[6], cb[7])
+    for m in range(2):
+        rows_here(4 + m)
+        arrive(jnp.logical_not(mover), vb.at[4 + m], r_vb.at[4 + m])
+
+    @pl.loop(0, 2)
+    def _(m):
+        col = carried(m, 2, cb[4 + m])
+        for r in range(2):
+            msend[m, r] = dot(pick, rb[4 + m, r, c], 1, 0)
+            row = carried(m, r, rb[4 + m, r, c])
+            acc[r] -= dot(row, col, 1, 1)
+            hp[r] -= dot(vb[4 + m], row, 1, 1)
+        hp[2] -= dot(vb[4 + m], col, 1, 1)
+
+    send(always, msend.at[xo // 2], mrecv.at[x // 2], r_ms.at[x // 2], lambda: dev(xo, zh, c, y, zl))
+    mrecv[x // 2] = msend[x // 2]
+
+    for k in (6, 7):
+        arrive(jnp.logical_not(mover) & jnp.logical_not(is_pd2), cb.at[k], r_cb.at[k])
+        rows_here(k)
+
+    def last_panel(w, high, low):
+        return solve_panel(hp[w] + high.astype(F32) + low.astype(F32), l0i[...])
+
+    col = last_panel(2, cb[6], cb[7])
     col = jnp.where(t == 2, 0.0, col).astype(BF16)
     for r in range(2):
         tile = row_tiles[r]
-        full = last_panel(rb[6, r, c], rb[7, r, c])
+        full = last_panel(r, rb[6, r, c], rb[7, r, c])
         full = jnp.where(lower | (tile != 2), full, 0.0).astype(BF16)
         root_out[r, 0] = dot(pick, full, 1, 0).astype(BF16)
         row = jnp.where(tile == 2, jnp.zeros_like(full), full)
@@ -441,9 +521,12 @@
         pltpu.VMEM((4, 2, 8, W), F32),
         pltpu.VMEM((2, 2, 8, W), F32),
         pltpu.VMEM((2, 2, 8, W), F32),
+        pltpu.VMEM((2, 2) + tile, F32),
+        pltpu.VMEM((6,) + tile, BF16),
+        pltpu.VMEM((3,) + tile, F32),
         dma((SENDS,)),
         dma((4, 2)), dma((2, 2)), dma, dma((8,)), dma((8, 2, 2)),
-        dma((3,)), dma, dma((3,)), dma((3,)), dma((4,)), dma((2,)),
+        dma((3,)), dma((2,)), dma((3,)), dma((3,)), dma((4,)), dma((2,)), dma((2, 2)), dma((6,)),
     ]
     return pl.pallas_call(
         kernel,
@@ -456,7 +539,7 @@
     )(leaf.reshape(8, W, W), middle.reshape(4, W, W), root.reshape(2, W, W), s2, s1, o2, o1)
 
 
-SENDS = 420
+SENDS = 480
 
 
 def solution(mesh):

time: 245 us -> 253 us (1.033)
  the two profiles are of different devices: /device:TPU:19 before, /device:TPU:247 now
where the time goes in v3:
time: 253 us; the launch traced here: 252 us
  Pallas kernels  240 us (95%)
  local copies, waits for them, and re-layouts  11.6 us (5%)
    pallas_call x1, Pallas kernels, per_device(): pl.pallas_call(kernel, out_shape=outs, in_specs=[vmem] * 5 + [smem] * 2,...  240 us
    unnamed x8, local copies, waits for them, and re-layouts  9.86 us

profile of v3, /device:TPU:247, one launch (start us, length us, event | category | flops | bytes accessed | tf_op | source)
XLA Modules:
  0.0 252.5 jit_solution(10273555043732583188)
XLA Ops:
  0.6 0.0 copy-start
  0.6 2.0 copy.20
  2.7 2.3 copy.19
  4.9 0.0 copy-done
  4.9 1.6 copy.18
  6.5 240.2 %window.1 = (bf16[8,1,8,256]{3,2,1,0:T(8,128)(2,1)}, bf16[4,1,8,256]{3,2,1,0:T(8,128)(2,1)}, bf16[2,1,8,256]{3,2,1,0:T(8,128)(2,1)}, bf16[2,256,1,256]{3,2,1,0:T(2,128)(2,1)}) custom-call(f32[8,256,256]{2,1,0:T(8,128)} %bitcast.9, f32[4,256,256]{2,1,0:T(8,128)} %bitcast.10, f32[2,256,256]{2,1,0:T(8,128)} %bitcast.11, s32[4,32,256]{2,1,0:T(8,128)} %s2_.1, ...), custom_call_target="tpu_custom_call" | custom-call | tf_op jit(solution)/shard_map/window/pallas_call | solution.py:531
  246.7 1.8 copy.11
  248.5 1.4 copy.24
  249.8 1.3 copy.25
  251.2 1.3 copy.26
Async XLA Ops:
  0.6 4.3 %copy-start = (f32[8,256,1,256]{3,2,1,0:T(1,128)S(1)}, f32[8,256,1,256]{3,2,1,0:T(1,128)}, u32[]{:S(2)}) copy-start(f32[8,256,1,256]{3,2,1,0:T(1,128)} %param.7) | copy-start | bytes 6291460

commit v4 on v3

--- a/solution.py
+++ b/solution.py
@@ -118,7 +118,6 @@
     is_pd1 = (zh == 0) & (c == 1) & (x % 2 == 0)
     is_pd2 = (x == 0) & (zh == 1) & (c == 0)
 
-    send((zh == 0) & (c == 1) & (x % 2 == 1), a2.at[0], pa, r_pa, lambda: dev(x - 1, zh, c, y, zl))
     xo = (x + 2) % 4
 
     def exchange(who):
@@ -141,7 +140,26 @@
                 send(who, rel.at[r, j], dst, recv, lambda xd=xd: dev(xd, zh, c, y, zl))
 
     late = t == 1
-    exchange(jnp.logical_not(late))
+    busy = is_pd0 & (t == 0)
+
+    barrier = pltpu.get_barrier_semaphore()
+
+    def signal(target):
+        pl.semaphore_signal(barrier, inc=1, device_id=target, device_id_type=MESH)
+
+    for apart in (1, 2, 3):
+        signal(dev((x + apart) % 4, zh, c, y, zl))
+        for cc in range(2):
+            signal(dev(x, zh, cc, (y + apart) % 4, zl))
+    signal(dev(x, zh, 1 - c, y, zl))
+    for cc in range(2):
+        signal(dev(x, 1 - zh, cc, y, zl))
+    for apart in (-3, -2, -1, 1, 2, 3):
+
+        @pl.when((zl + apart >= 0) & (zl + apart < 8))
+        def _(apart=apart):
+            signal(dev(x, zh, c, y, zl + apart))
+
     for r in range(2):
         ta2[x, r] = a2[4 * r + x]
         ta1[x // 2, r] = a1[2 * r + x // 2]
@@ -187,12 +205,15 @@
         for other in (1, 3, 2):
             send(who & (y == 0), ref, ref, recv, lambda o=other: dev(x, 0, ch, o, zl))
 
-    busy = is_pd0 & (t == 0)
+    @pl.when(busy)
+    def _():
+        inverse_factor(a2.at[0], li)
+
+    pl.semaphore_wait(barrier, 12 + jnp.minimum(zl, 3) + jnp.minimum(7 - zl, 3))
+
+    send((zh == 0) & (c == 1) & (x % 2 == 1), a2.at[0], pa, r_pa, lambda: dev(x - 1, zh, c, y, zl))
+    exchange(jnp.logical_not(late | busy))
     pass_on(jnp.logical_not(late | busy))
-
-    @pl.when(is_pd0 & (t == 0))
-    def _():
-        inverse_factor(a2.at[0], li)
 
     @pl.when(jnp.logical_not(is_pd0 & (t == 0)))
     def _():
@@ -201,6 +222,7 @@
     for part, recv in pieces(li, r_li):
         fan_out(is_pd0, part, recv, 0, 0)
 
+    exchange(busy)
     pass_on(busy)
 
     @pl.when(is_pd0)
@@ -216,6 +238,11 @@
 
     def line(r):
         return mover & (y == x // 2 + 2 * r)
+
+    def halves(k, ref, recv):
+        if k in (4, 5):
+            return ((ref.at[:half], recv.at[0]), (ref.at[half:], recv.at[1]))
+        return ((ref, recv.at[0]),)
 
     def row_stage(k):
         z0 = 4 * (x % 2) + 2 * zh
@@ -223,22 +250,24 @@
             for r in range(2):
                 at = z0 + cc
                 source = line(r) & (zl == at)
-                ref, recv = rb.at[k, r, cc], r_rb.at[k, r, cc]
+                ref = rb.at[k, r, cc]
 
                 @pl.when(source)
                 def _():
                     rb[k, r, cc] = cb[k]
 
-                arrive(line(r) & (zl != at), ref, recv)
-                send(line(r) & (zl >= at) & (zl < 7), ref, ref, recv, lambda: dev(x, zh, c, y, zl + 1))
-                send(line(r) & (zl <= at) & (zl > 0), ref, ref, recv, lambda: dev(x, zh, c, y, zl - 1))
-                for apart in (1, 3, 2):
-                    send(line(r), ref, ref, recv, lambda a=apart, cc=cc: dev(x, zh, cc, (y + a) % 4, zl))
-                send(line(r) & (c != cc), ref, ref, recv, lambda: dev(x, zh, 1 - c, y, zl))
+                for part, recv in halves(k, ref, r_rb.at[k, r, cc]):
+                    arrive(line(r) & (zl != at), part, recv)
+                    send(line(r) & (zl >= at) & (zl < 7), part, part, recv, lambda: dev(x, zh, c, y, zl + 1))
+                    send(line(r) & (zl <= at) & (zl > 0), part, part, recv, lambda: dev(x, zh, c, y, zl - 1))
+                    for apart in (1, 3, 2):
+                        send(line(r), part, part, recv, lambda a=apart, cc=cc: dev(x, zh, cc, (y + a) % 4, zl))
+                    send(line(r) & (c != cc), part, part, recv, lambda: dev(x, zh, 1 - c, y, zl))
 
     def rows_here(k):
         for r in range(2):
-            arrive(jnp.logical_not(line(r)), rb.at[k, r, c], r_rb.at[k, r, c])
+            for part, recv in halves(k, rb.at[k, r, c], r_rb.at[k, r, c]):
+                arrive(jnp.logical_not(line(r)), part, recv)
 
     for l in range(4):
         send(is_pd0 & (x == l), cb.at[l], cb.at[l], r_cb.at[l], lambda: dev(x, 1, 1, y, zl))
@@ -361,7 +390,7 @@
     for l in range(4):
         pivot_stage(l)
     pass_on(late & mover)
-    root_tiles(jnp.logical_not(early))
+    root_tiles(jnp.logical_not(early | late))
     for k in (6, 7):
         column_stage(k, x == 0, always & False, (zh == 1) & (x == 0))
     for k in (6, 7):
@@ -393,6 +422,7 @@
         row_stage(4 + m)
     for m in range(2):
         pivot_stage(4 + m)
+    root_tiles(late & jnp.logical_not(early))
     for k in range(6):
         arrive(mover & (y != 0), vb.at[k], r_vb.at[k])
         send(mover & (y != 0), vb.at[k], vb.at[k], r_vb.at[k], lambda: dev(x, zh, 1 - c, y, zl))
@@ -471,7 +501,7 @@
         full = jnp.where(lower | (tile != 2), full, 0.0).astype(BF16)
         root_out[r, 0] = dot(pick, full, 1, 0).astype(BF16)
         row = jnp.where(tile == 2, jnp.zeros_like(full), full)
-        schur_out[r, :, 0, :] = (acc[r] - dot(row, col, 1, 1)).astype(BF16)
+        schur_out[r] = (acc[r] - dot(row, col, 1, 1)).astype(BF16)
 
     for s in range(4):
         arrive(x != s, precv.at[s], r_ps.at[s])
@@ -499,7 +529,7 @@
         jax.ShapeDtypeStruct((8, 1, 8, W), BF16),
         jax.ShapeDtypeStruct((4, 1, 8, W), BF16),
         jax.ShapeDtypeStruct((2, 1, 8, W), BF16),
-        jax.ShapeDtypeStruct((2, W, 1, W), BF16),
+        jax.ShapeDtypeStruct((2, W, W), BF16),
     ]
     tile = (W, W)
     scratch = [
@@ -525,21 +555,22 @@
         pltpu.VMEM((6,) + tile, BF16),
         pltpu.VMEM((3,) + tile, F32),
         dma((SENDS,)),
-        dma((4, 2)), dma((2, 2)), dma, dma((8,)), dma((8, 2, 2)),
+        dma((4, 2)), dma((2, 2)), dma, dma((8,)), dma((8, 2, 2, 2)),
         dma((3,)), dma((2,)), dma((3,)), dma((3,)), dma((4,)), dma((2,)), dma((2, 2)), dma((6,)),
     ]
-    return pl.pallas_call(
+    *panels, schur = pl.pallas_call(
         kernel,
         out_shape=outs,
         in_specs=[vmem] * 5 + [smem] * 2,
         out_specs=[vmem] * 4,
         scratch_shapes=scratch,
-        compiler_params=pltpu.CompilerParams(has_side_effects=True, vmem_limit_bytes=60 * 2**20),
+        compiler_params=pltpu.CompilerParams(has_side_effects=True, collective_id=0, vmem_limit_bytes=60 * 2**20),
         name="window",
     )(leaf.reshape(8, W, W), middle.reshape(4, W, W), root.reshape(2, W, W), s2, s1, o2, o1)
-
-
-SENDS = 480
+    return (*panels, schur.reshape(2, W, 1, W))
+
+
+SENDS = 560
 
 
 def solution(mesh):

time: 253 us -> 232 us (0.917)
  Pallas kernels: 240 us -> 220 us
    pallas_call x1, Pallas kernels: 240 us -> 220 us  [per_device(): pl.pallas_call(kernel, out_shape=outs, in_specs=[vmem] * 5 + [smem] * 2,...]
    unnamed x8 -> x9, local copies, waits for them, and re-layouts: 9.86 us -> 11.5 us
where the time goes in v4:
time: 232 us
  Pallas kernels  220 us (95%)
  local copies, waits for them, and re-layouts  11.5 us (5%)
    pallas_call x1, Pallas kernels, per_device(): pl.pallas_call(kernel, out_shape=outs, in_specs=[vmem] * 5 + [smem] * 2,...  220 us
    unnamed x9, local copies, waits for them, and re-layouts  11.5 us

profile of v4, /device:TPU:247, one launch (start us, length us, event | category | flops | bytes accessed | tf_op | source)
XLA Modules:
  0.0 231.7 jit_solution(2336171515252841957)
XLA Ops:
  0.6 0.0 copy-start
  0.6 2.0 copy.20
  2.7 2.3 copy.19
  4.9 0.0 copy-done
  4.9 1.6 copy.18
  6.5 219.5 %window.1 = (bf16[8,1,8,256]{3,2,1,0:T(8,128)(2,1)}, bf16[4,1,8,256]{3,2,1,0:T(8,128)(2,1)}, bf16[2,1,8,256]{3,2,1,0:T(8,128)(2,1)}, bf16[2,256,256]{2,1,0:T(8,128)(2,1)}) custom-call(f32[8,256,256]{2,1,0:T(8,128)} %bitcast.12, f32[4,256,256]{2,1,0:T(8,128)} %bitcast.13, f32[2,256,256]{2,1,0:T(8,128)} %bitcast.14, s32[4,32,256]{2,1,0:T(8,128)} %s2_.1, ...), custom_call_target="tpu_custom_call" | custom-call | tf_op jit(solution)/shard_map/window/pallas_call | solution.py:561
  226.0 1.4 copy.25
  227.4 1.3 copy.26
  228.7 1.3 copy.27
  230.0 1.7 copy.28
Async XLA Ops:
  0.6 4.3 %copy-start = (f32[8,256,1,256]{3,2,1,0:T(1,128)S(1)}, f32[8,256,1,256]{3,2,1,0:T(1,128)}, u32[]{:S(2)}) copy-start(f32[8,256,1,256]{3,2,1,0:T(1,128)} %param.7) | copy-start | bytes 6291460

commit v5 on v4

--- a/solution.py
+++ b/solution.py
@@ -76,8 +76,8 @@
 def kernel(
     a2, a1, a0, s2, s1, o2, o1,
     leaf_out, mid_out, root_out, schur_out,
-    ta2, ta1, pa, cb, rb, li, yb, l1i, l0i, hs, pl2, pm1, acc, ts, psend, precv, msend, mrecv, rel, vb, hp,
-    send_sem, r_ta2, r_ta1, r_pa, r_cb, r_rb, r_li, r_yb, r_l1, r_l0, r_ps, r_ms, r_rel, r_vb,
+    ta2, ta1, pa, cb, rb, li, yb, l1i, l0i, hs, pl2, pm1, acc, ts, psend, precv, msend, mrecv, rel, vb, hp, vx,
+    send_sem, r_ta2, r_ta1, r_pa, r_cb, r_rb, r_li, r_yb, r_l1, r_l0, r_ps, r_ms, r_rel, r_vb, r_vx,
 ):
     cube, t = lax.axis_index("cube"), lax.axis_index("tile")
     x, zh, c = cube // 4, (cube // 2) % 2, cube % 2
@@ -385,44 +385,65 @@
         send(mine, cb.at[4 + m], cb.at[4 + m], r_cb.at[4 + m], lambda: dev(x, 0, 0, y, zl))
         send(mine, cb.at[4 + m], cb.at[4 + m], r_cb.at[4 + m], lambda: dev(x, 1, 1, y, zl))
 
+    hop = is_pd1 & (t == 2)
+    send(hop & (x == 2), cb.at[5], vx.at[1], r_vx.at[1], lambda: dev(0, 0, 1, y, zl))
+    send(hop & (x == 0), cb.at[4], vx.at[0], r_vx.at[0], lambda: dev(0, 1, 0, y, zl))
+    arrive(hop & (x == 0), vx.at[1], r_vx.at[1])
+    send(hop & (x == 0), vx.at[1], vx.at[1], r_vx.at[1], lambda: dev(0, 1, 0, y, zl))
+    root_tiles(jnp.logical_not(early | mover))
+
+    root = is_pd2 & (t == 2)
+
+    for i in range(2):
+        arrive(root, vx.at[i], r_vx.at[i])
+
+    @pl.when(root)
+    def _():
+        total = acc[0]
+        for k in range(6):
+            block = column_of(k) if k < 4 else carried(k - 4, 2, vx[k - 4])
+            total = total - dot(block, block, 1, 1)
+        hs[...] = total
+        inverse_factor(hs, l0i)
+
+    @pl.when(jnp.logical_not(root))
+    def _():
+        clear_upper(l0i)
+
+    still = jnp.logical_not(mover)
+    two = still & (y == 0) & (zl == 2)
+    for part, recv in pieces(l0i, r_l0):
+        arrive(still & jnp.logical_not(root), part, recv)
+        send(two & (x == 0) & (zh == 1), part, part, recv, lambda: dev(0, 0, 1, 0, 2))
+        for other in (1, 3, 2):
+            send(two & (x == 0), part, part, recv, lambda o=other: dev(o, zh, c, 0, 2))
+        for other in (1, 3, 2):
+            send(two, part, part, recv, lambda o=other: dev(x, zh, c, o, 2))
+        for at, other in TREES[2]:
+            send(still & (zl == at), part, part, recv, lambda o=other: dev(x, zh, c, y, o))
+        send(still, part, part, recv, lambda: dev(x, zh, 1 - c, y, zl))
+
+    for k in (6, 7):
+        column_stage(k, x == 0, always & False, (zh == 1) & (x == 0))
+    for k in (6, 7):
+        row_stage(k)
     for l in range(4):
         row_stage(l)
     for l in range(4):
         pivot_stage(l)
     pass_on(late & mover)
-    root_tiles(jnp.logical_not(early | late))
-    for k in (6, 7):
-        column_stage(k, x == 0, always & False, (zh == 1) & (x == 0))
-    for k in (6, 7):
-        row_stage(k)
+    ahead = mover & jnp.logical_not(line(0) | line(1) | late)
+    root_tiles(ahead)
     for m in range(2):
         column_stage(4 + m, x == 2 * m, always & False, (zh == 0) & (x == 2 * m))
     for m in range(2):
         arrive(jnp.logical_not(mover) & jnp.logical_not(is_pd1 & (x == 2 * m)), cb.at[4 + m], r_cb.at[4 + m])
 
-    root = is_pd2 & (t == 2)
-
-    @pl.when(root)
-    def _():
-        total = acc[0]
-        for k in range(6):
-            block = column_of(k)
-            total = total - dot(block, block, 1, 1)
-        hs[...] = total
-        inverse_factor(hs, l0i)
-
-    @pl.when(jnp.logical_not(root))
-    def _():
-        clear_upper(l0i)
-
-    for part, recv in pieces(l0i, r_l0):
-        send(root, part, part, recv, lambda: dev(0, 1, 1, 0, 2))
-
     for m in range(2):
         row_stage(4 + m)
     for m in range(2):
         pivot_stage(4 + m)
-    root_tiles(late & jnp.logical_not(early))
+    root_tiles(mover & jnp.logical_not(ahead))
     for k in range(6):
         arrive(mover & (y != 0), vb.at[k], r_vb.at[k])
         send(mover & (y != 0), vb.at[k], vb.at[k], r_vb.at[k], lambda: dev(x, zh, 1 - c, y, zl))
@@ -454,21 +475,6 @@
         send(always, psend.at[xd], precv.at[x], r_ps.at[x], lambda xd=xd: dev(xd, zh, c, y, zl))
     precv[x] = psend[x]
 
-    two = mover & (y == 0) & (zl == 2)
-    for part, recv in pieces(l0i, r_l0):
-        arrive(jnp.logical_not(root), part, recv)
-        send(two & (x == 0) & (zh == 1), part, part, recv, lambda: dev(0, 0, 0, 0, 2))
-        for other in (1, 3, 2):
-            send(two & (x == 0), part, part, recv, lambda o=other: dev(o, zh, c, 0, 2))
-        for other in (1, 3, 2):
-            send(two, part, part, recv, lambda o=other: dev(x, zh, c, o, 2))
-        for at, other in TREES[2]:
-            send(mover & (zl == at), part, part, recv, lambda o=other: dev(x, zh, c, y, o))
-        send(
-            mover & jnp.logical_not((x == 0) & (zh == 1) & (t == 2)),
-            part, part, recv, lambda: dev(x, zh, 1 - c, y, zl),
-        )
-
     for m in range(2):
         rows_here(4 + m)
         arrive(jnp.logical_not(mover), vb.at[4 + m], r_vb.at[4 + m])
@@ -489,6 +495,9 @@
     for k in (6, 7):
         arrive(jnp.logical_not(mover) & jnp.logical_not(is_pd2), cb.at[k], r_cb.at[k])
         rows_here(k)
+
+    for part, recv in pieces(l0i, r_l0):
+        arrive(mover, part, recv)
 
     def last_panel(w, high, low):
         return solve_panel(hp[w] + high.astype(F32) + low.astype(F32), l0i[...])
@@ -554,9 +563,10 @@
         pltpu.VMEM((2, 2) + tile, F32),
         pltpu.VMEM((6,) + tile, BF16),
         pltpu.VMEM((3,) + tile, F32),
+        pltpu.VMEM((2,) + tile, BF16),
         dma((SENDS,)),
         dma((4, 2)), dma((2, 2)), dma, dma((8,)), dma((8, 2, 2, 2)),
-        dma((3,)), dma((2,)), dma((3,)), dma((3,)), dma((4,)), dma((2,)), dma((2, 2)), dma((6,)),
+        dma((3,)), dma((2,)), dma((3,)), dma((3,)), dma((4,)), dma((2,)), dma((2, 2)), dma((6,)), dma((2,)),
     ]
     *panels, schur = pl.pallas_call(
         kernel,

time: 232 us -> 223 us (0.961)
  the two profiles are of different devices: /device:TPU:247 before, /device:TPU:503 now
where the time goes in v5:
time: 223 us
  Pallas kernels  211 us (95%)
  local copies, waits for them, and re-layouts  11.5 us (5%)
    pallas_call x1, Pallas kernels, per_device(): pl.pallas_call(kernel, out_shape=outs, in_specs=[vmem] * 5 + [smem] * 2,...  211 us
    unnamed x9, local copies, waits for them, and re-layouts  11.5 us

profile of v5, /device:TPU:503, one launch (start us, length us, event | category | flops | bytes accessed | tf_op | source)
XLA Modules:
  0.0 223.0 jit_solution(14313045380862721720)
XLA Ops:
  0.6 0.0 copy-start
  0.6 2.0 copy.20
  2.7 2.3 %copy.19 = f32[4,256,1,256]{3,1,2,0:T(8,128)} copy(f32[4,256,1,256]{3,2,1,0:T(1,128)} %param.8) | data formatting | bytes 2097152
  4.9 0.0 copy-done
  4.9 1.6 copy.18
  6.5 210.9 %window.1 = (bf16[8,1,8,256]{3,2,1,0:T(8,128)(2,1)}, bf16[4,1,8,256]{3,2,1,0:T(8,128)(2,1)}, bf16[2,1,8,256]{3,2,1,0:T(8,128)(2,1)}, bf16[2,256,256]{2,1,0:T(8,128)(2,1)}) custom-call(f32[8,256,256]{2,1,0:T(8,128)} %bitcast.12, f32[4,256,256]{2,1,0:T(8,128)} %bitcast.13, f32[2,256,256]{2,1,0:T(8,128)} %bitcast.14, s32[4,32,256]{2,1,0:T(8,128)} %s2_.1, ...), custom_call_target="tpu_custom_call" | custom-call | tf_op jit(solution)/shard_map/window/pallas_call | solution.py:571
  217.4 1.4 copy.25
  218.7 1.3 copy.26
  220.1 1.3 copy.27
  221.4 1.7 copy.28
Async XLA Ops:
  0.6 4.3 %copy-start = (f32[8,256,1,256]{3,2,1,0:T(1,128)S(1)}, f32[8,256,1,256]{3,2,1,0:T(1,128)}, u32[]{:S(2)}) copy-start(f32[8,256,1,256]{3,2,1,0:T(1,128)} %param.7) | copy-start | bytes 6291460

commit v6 on v5

--- a/solution.py
+++ b/solution.py
@@ -84,6 +84,7 @@
     y, zl = t // 8, t % 8
     g = 2 * zh + c
     mover = c == zh
+    still = c != zh
     pending = []
 
     def dev(x_, zh_, c_, y_, zl_):
@@ -230,14 +231,17 @@
         panel = solve_panel(a2[0], li[...])
         cb[x] = jnp.where(lower | (t != 0), panel, 0.0).astype(BF16)
 
+    def carrier(k):
+        return still if k in (4, 5) else mover
+
     def column_stage(k, holder, own, known):
-        arrive(mover & jnp.logical_not(own), cb.at[k], r_cb.at[k])
-        send(mover & jnp.logical_not(known), cb.at[k], cb.at[k], r_cb.at[k], lambda: dev(x, zh, 1 - c, y, zl))
+        arrive(carrier(k) & jnp.logical_not(own), cb.at[k], r_cb.at[k])
+        send(carrier(k) & jnp.logical_not(known), cb.at[k], cb.at[k], r_cb.at[k], lambda: dev(x, zh, 1 - c, y, zl))
         for apart in (1, 3, 2):
-            send(mover & holder, cb.at[k], cb.at[k], r_cb.at[k], lambda a=apart: dev((x + a) % 4, zh, c, y, zl))
-
-    def line(r):
-        return mover & (y == x // 2 + 2 * r)
+            send(carrier(k) & holder, cb.at[k], cb.at[k], r_cb.at[k], lambda a=apart: dev((x + a) % 4, zh, c, y, zl))
+
+    def line(r, k=0):
+        return carrier(k) & (y == x // 2 + 2 * r)
 
     def halves(k, ref, recv):
         if k in (4, 5):
@@ -249,7 +253,7 @@
         for cc in range(2):
             for r in range(2):
                 at = z0 + cc
-                source = line(r) & (zl == at)
+                source = line(r, k) & (zl == at)
                 ref = rb.at[k, r, cc]
 
                 @pl.when(source)
@@ -257,17 +261,17 @@
                     rb[k, r, cc] = cb[k]
 
                 for part, recv in halves(k, ref, r_rb.at[k, r, cc]):
-                    arrive(line(r) & (zl != at), part, recv)
-                    send(line(r) & (zl >= at) & (zl < 7), part, part, recv, lambda: dev(x, zh, c, y, zl + 1))
-                    send(line(r) & (zl <= at) & (zl > 0), part, part, recv, lambda: dev(x, zh, c, y, zl - 1))
+                    arrive(line(r, k) & (zl != at), part, recv)
+                    send(line(r, k) & (zl >= at) & (zl < 7), part, part, recv, lambda: dev(x, zh, c, y, zl + 1))
+                    send(line(r, k) & (zl <= at) & (zl > 0), part, part, recv, lambda: dev(x, zh, c, y, zl - 1))
                     for apart in (1, 3, 2):
-                        send(line(r), part, part, recv, lambda a=apart, cc=cc: dev(x, zh, cc, (y + a) % 4, zl))
-                    send(line(r) & (c != cc), part, part, recv, lambda: dev(x, zh, 1 - c, y, zl))
+                        send(line(r, k), part, part, recv, lambda a=apart, cc=cc: dev(x, zh, cc, (y + a) % 4, zl))
+                    send(line(r, k) & (c != cc), part, part, recv, lambda: dev(x, zh, 1 - c, y, zl))
 
     def rows_here(k):
         for r in range(2):
             for part, recv in halves(k, rb.at[k, r, c], r_rb.at[k, r, c]):
-                arrive(jnp.logical_not(line(r)), part, recv)
+                arrive(jnp.logical_not(line(r, k)), part, recv)
 
     for l in range(4):
         send(is_pd0 & (x == l), cb.at[l], cb.at[l], r_cb.at[l], lambda: dev(x, 1, 1, y, zl))
@@ -322,11 +326,11 @@
         return carried(k - 4, 2, cb[k])
 
     def pivot_stage(k):
-        @pl.when(mover & (t == 2))
+        @pl.when(carrier(k) & (t == 2))
         def _():
             vb[k] = column_of(k)
 
-        zero = mover & (y == 0)
+        zero = carrier(k) & (y == 0)
         arrive(zero & (zl != 2), vb.at[k], r_vb.at[k])
         send(zero & (zl >= 2) & (zl < 7), vb.at[k], vb.at[k], r_vb.at[k], lambda: dev(x, zh, c, y, zl + 1))
         send(zero & (zl <= 2) & (zl > 0), vb.at[k], vb.at[k], r_vb.at[k], lambda: dev(x, zh, c, y, zl - 1))
@@ -382,8 +386,7 @@
 
     for m in range(2):
         mine = is_pd1 & (x == 2 * m)
-        send(mine, cb.at[4 + m], cb.at[4 + m], r_cb.at[4 + m], lambda: dev(x, 0, 0, y, zl))
-        send(mine, cb.at[4 + m], cb.at[4 + m], r_cb.at[4 + m], lambda: dev(x, 1, 1, y, zl))
+        send(mine, cb.at[4 + m], cb.at[4 + m], r_cb.at[4 + m], lambda: dev(x, 1, 0, y, zl))
 
     hop = is_pd1 & (t == 2)
     send(hop & (x == 2), cb.at[5], vx.at[1], r_vx.at[1], lambda: dev(0, 0, 1, y, zl))
@@ -409,19 +412,6 @@
     @pl.when(jnp.logical_not(root))
     def _():
         clear_upper(l0i)
-
-    still = jnp.logical_not(mover)
-    two = still & (y == 0) & (zl == 2)
-    for part, recv in pieces(l0i, r_l0):
-        arrive(still & jnp.logical_not(root), part, recv)
-        send(two & (x == 0) & (zh == 1), part, part, recv, lambda: dev(0, 0, 1, 0, 2))
-        for other in (1, 3, 2):
-            send(two & (x == 0), part, part, recv, lambda o=other: dev(o, zh, c, 0, 2))
-        for other in (1, 3, 2):
-            send(two, part, part, recv, lambda o=other: dev(x, zh, c, o, 2))
-        for at, other in TREES[2]:
-            send(still & (zl == at), part, part, recv, lambda o=other: dev(x, zh, c, y, o))
-        send(still, part, part, recv, lambda: dev(x, zh, 1 - c, y, zl))
 
     for k in (6, 7):
         column_stage(k, x == 0, always & False, (zh == 1) & (x == 0))
@@ -432,21 +422,33 @@
     for l in range(4):
         pivot_stage(l)
     pass_on(late & mover)
-    ahead = mover & jnp.logical_not(line(0) | line(1) | late)
-    root_tiles(ahead)
+    root_tiles(mover & jnp.logical_not(late))
+    two = mover & (y == 0) & (zl == 2)
+    for part, recv in pieces(l0i, r_l0):
+        send(root, part, part, recv, lambda: dev(0, 1, 1, 0, 2))
+        arrive(mover, part, recv)
+        send(two & (x == 0) & (zh == 1), part, part, recv, lambda: dev(0, 0, 0, 0, 2))
+        for other in (1, 3, 2):
+            send(two & (x == 0), part, part, recv, lambda o=other: dev(o, zh, c, 0, 2))
+        for other in (1, 3, 2):
+            send(two, part, part, recv, lambda o=other: dev(x, zh, c, o, 2))
+        for at, other in TREES[2]:
+            send(mover & (zl == at), part, part, recv, lambda o=other: dev(x, zh, c, y, o))
+        send(
+            mover & jnp.logical_not((x == 0) & (zh == 1) & (t == 2)),
+            part, part, recv, lambda: dev(x, zh, 1 - c, y, zl),
+        )
+    root_tiles(mover & late)
     for m in range(2):
-        column_stage(4 + m, x == 2 * m, always & False, (zh == 0) & (x == 2 * m))
-    for m in range(2):
-        arrive(jnp.logical_not(mover) & jnp.logical_not(is_pd1 & (x == 2 * m)), cb.at[4 + m], r_cb.at[4 + m])
-
+        column_stage(4 + m, x == 2 * m, is_pd1 & (x == 2 * m), always & False)
     for m in range(2):
         row_stage(4 + m)
     for m in range(2):
         pivot_stage(4 + m)
-    root_tiles(mover & jnp.logical_not(ahead))
     for k in range(6):
-        arrive(mover & (y != 0), vb.at[k], r_vb.at[k])
-        send(mover & (y != 0), vb.at[k], vb.at[k], r_vb.at[k], lambda: dev(x, zh, 1 - c, y, zl))
+        relay = carrier(k) & (y != 0)
+        arrive(relay, vb.at[k], r_vb.at[k])
+        send(relay, vb.at[k], vb.at[k], r_vb.at[k], lambda: dev(x, zh, 1 - c, y, zl))
     for l in range(4):
         rows_here(l)
     for k in range(4):
@@ -477,7 +479,8 @@
 
     for m in range(2):
         rows_here(4 + m)
-        arrive(jnp.logical_not(mover), vb.at[4 + m], r_vb.at[4 + m])
+        arrive(mover, cb.at[4 + m], r_cb.at[4 + m])
+        arrive(mover, vb.at[4 + m], r_vb.at[4 + m])
 
     @pl.loop(0, 2)
     def _(m):
@@ -497,7 +500,7 @@
         rows_here(k)
 
     for part, recv in pieces(l0i, r_l0):
-        arrive(mover, part, recv)
+        arrive(still & jnp.logical_not(root), part, recv)
 
     def last_panel(w, high, low):
         return solve_panel(hp[w] + high.astype(F32) + low.astype(F32), l0i[...])

time: 223 us -> 216 us (0.969)
  the two profiles are of different devices: /device:TPU:503 before, /device:TPU:500 now
where the time goes in v6:
time: 216 us; the launch traced here: 215 us
  Pallas kernels  203 us (94%)
  local copies, waits for them, and re-layouts  11.5 us (5%)
    pallas_call x1, Pallas kernels, per_device(): pl.pallas_call(kernel, out_shape=outs, in_specs=[vmem] * 5 + [smem] * 2,...  203 us
    unnamed x9, local copies, waits for them, and re-layouts  11.5 us

profile of v6, /device:TPU:500, one launch (start us, length us, event | category | flops | bytes accessed | tf_op | source)
XLA Modules:
  0.0 215.1 jit_solution(17743047126109513614)
XLA Ops:
  0.6 0.0 copy-start
  0.6 2.0 copy.20
  2.7 2.3 %copy.19 = f32[4,256,1,256]{3,1,2,0:T(8,128)} copy(f32[4,256,1,256]{3,2,1,0:T(1,128)} %param.8) | data formatting | bytes 2097152
  4.9 0.0 copy-done
  4.9 1.6 copy.18
  6.5 203.0 %window.1 = (bf16[8,1,8,256]{3,2,1,0:T(8,128)(2,1)}, bf16[4,1,8,256]{3,2,1,0:T(8,128)(2,1)}, bf16[2,1,8,256]{3,2,1,0:T(8,128)(2,1)}, bf16[2,256,256]{2,1,0:T(8,128)(2,1)}) custom-call(f32[8,256,256]{2,1,0:T(8,128)} %bitcast.12, f32[4,256,256]{2,1,0:T(8,128)} %bitcast.13, f32[2,256,256]{2,1,0:T(8,128)} %bitcast.14, s32[4,32,256]{2,1,0:T(8,128)} %s2_.1, ...), custom_call_target="tpu_custom_call" | custom-call | tf_op jit(solution)/shard_map/window/pallas_call | solution.py:574
  209.5 1.4 copy.25
  210.9 1.3 copy.26
  212.2 1.3 copy.27
  213.5 1.7 copy.28
Async XLA Ops:
  0.6 4.3 %copy-start = (f32[8,256,1,256]{3,2,1,0:T(1,128)S(1)}, f32[8,256,1,256]{3,2,1,0:T(1,128)}, u32[]{:S(2)}) copy-start(f32[8,256,1,256]{3,2,1,0:T(1,128)} %param.7) | copy-start | bytes 6291460

commit v7 on v6

--- a/solution.py
+++ b/solution.py
@@ -85,26 +85,34 @@
     g = 2 * zh + c
     mover = c == zh
     still = c != zh
-    pending = []
+    pending, used = {}, []
 
     def dev(x_, zh_, c_, y_, zl_):
         return (x_ * 4 + zh_ * 2 + c_, y_ * 8 + zl_)
 
-    def send(pred, src, dst, recv, target):
-        index = len(pending)
-
-        def make():
-            return pltpu.make_async_remote_copy(
-                src_ref=src, dst_ref=dst, send_sem=send_sem.at[index], recv_sem=recv,
-                device_id=target(), device_id_type=MESH,
-            )
-
-        assert index < SENDS
-        pending.append((pred, make))
+    def send_all(pred, copies, outer=None):
+        makers = []
+        for src, dst, recv, target in copies:
+            index = len(used)
+            assert index < SENDS
+            used.append(index)
+
+            def make(src=src, dst=dst, recv=recv, target=target, index=index):
+                return pltpu.make_async_remote_copy(
+                    src_ref=src, dst_ref=dst, send_sem=send_sem.at[index], recv_sem=recv,
+                    device_id=target(), device_id_type=MESH,
+                )
+
+            makers.append(make)
+        pending.setdefault(outer and outer[0], (outer and outer[1], []))[1].append((pred, makers))
 
         @pl.when(pred)
         def _():
-            make().start()
+            for make in makers:
+                make().start()
+
+    def send(pred, src, dst, recv, target, outer=None):
+        send_all(pred, [(src, dst, recv, target)], outer)
 
     def arrive(pred, dst, recv):
         @pl.when(pred)
@@ -203,8 +211,7 @@
         arrive(who & ((y != 0) | (zl != root_zl)), ref, recv)
         for at, other in TREES[root_zl]:
             send(who & (y == 0) & (zl == at), ref, ref, recv, lambda o=other: dev(x, 0, ch, 0, o))
-        for other in (1, 3, 2):
-            send(who & (y == 0), ref, ref, recv, lambda o=other: dev(x, 0, ch, o, zl))
+        send_all(who & (y == 0), [(ref, ref, recv, lambda o=other: dev(x, 0, ch, o, zl)) for other in (1, 3, 2)])
 
     @pl.when(busy)
     def _():
@@ -237,8 +244,7 @@
     def column_stage(k, holder, own, known):
         arrive(carrier(k) & jnp.logical_not(own), cb.at[k], r_cb.at[k])
         send(carrier(k) & jnp.logical_not(known), cb.at[k], cb.at[k], r_cb.at[k], lambda: dev(x, zh, 1 - c, y, zl))
-        for apart in (1, 3, 2):
-            send(carrier(k) & holder, cb.at[k], cb.at[k], r_cb.at[k], lambda a=apart: dev((x + a) % 4, zh, c, y, zl))
+        send_all(carrier(k) & holder, [(cb.at[k], cb.at[k], r_cb.at[k], lambda a=apart: dev((x + a) % 4, zh, c, y, zl)) for apart in (1, 3, 2)])
 
     def line(r, k=0):
         return carrier(k) & (y == x // 2 + 2 * r)
@@ -260,13 +266,13 @@
                 def _():
                     rb[k, r, cc] = cb[k]
 
+                outer = ((r, k in (4, 5)), line(r, k))
                 for part, recv in halves(k, ref, r_rb.at[k, r, cc]):
                     arrive(line(r, k) & (zl != at), part, recv)
-                    send(line(r, k) & (zl >= at) & (zl < 7), part, part, recv, lambda: dev(x, zh, c, y, zl + 1))
-                    send(line(r, k) & (zl <= at) & (zl > 0), part, part, recv, lambda: dev(x, zh, c, y, zl - 1))
-                    for apart in (1, 3, 2):
-                        send(line(r, k), part, part, recv, lambda a=apart, cc=cc: dev(x, zh, cc, (y + a) % 4, zl))
-                    send(line(r, k) & (c != cc), part, part, recv, lambda: dev(x, zh, 1 - c, y, zl))
+                    send(line(r, k) & (zl >= at) & (zl < 7), part, part, recv, lambda: dev(x, zh, c, y, zl + 1), outer)
+                    send(line(r, k) & (zl <= at) & (zl > 0), part, part, recv, lambda: dev(x, zh, c, y, zl - 1), outer)
+                    send_all(line(r, k), [(part, part, recv, lambda a=apart, cc=cc: dev(x, zh, cc, (y + a) % 4, zl)) for apart in (1, 3, 2)], outer)
+                    send(line(r, k) & (c != cc), part, part, recv, lambda: dev(x, zh, 1 - c, y, zl), outer)
 
     def rows_here(k):
         for r in range(2):
@@ -334,8 +340,7 @@
         arrive(zero & (zl != 2), vb.at[k], r_vb.at[k])
         send(zero & (zl >= 2) & (zl < 7), vb.at[k], vb.at[k], r_vb.at[k], lambda: dev(x, zh, c, y, zl + 1))
         send(zero & (zl <= 2) & (zl > 0), vb.at[k], vb.at[k], r_vb.at[k], lambda: dev(x, zh, c, y, zl - 1))
-        for other in (1, 3, 2):
-            send(zero, vb.at[k], vb.at[k], r_vb.at[k], lambda o=other: dev(x, zh, c, o, zl))
+        send_all(zero, [(vb.at[k], vb.at[k], r_vb.at[k], lambda o=other: dev(x, zh, c, o, zl)) for other in (1, 3, 2)])
         send(zero, vb.at[k], vb.at[k], r_vb.at[k], lambda: dev(x, zh, 1 - c, y, zl))
 
     for l in range(4):
@@ -428,10 +433,8 @@
         send(root, part, part, recv, lambda: dev(0, 1, 1, 0, 2))
         arrive(mover, part, recv)
         send(two & (x == 0) & (zh == 1), part, part, recv, lambda: dev(0, 0, 0, 0, 2))
-        for other in (1, 3, 2):
-            send(two & (x == 0), part, part, recv, lambda o=other: dev(o, zh, c, 0, 2))
-        for other in (1, 3, 2):
-            send(two, part, part, recv, lambda o=other: dev(x, zh, c, o, 2))
+        send_all(two & (x == 0), [(part, part, recv, lambda o=other: dev(o, zh, c, 0, 2)) for other in (1, 3, 2)])
+        send_all(two, [(part, part, recv, lambda o=other: dev(x, zh, c, o, 2)) for other in (1, 3, 2)])
         for at, other in TREES[2]:
             send(mover & (zl == at), part, part, recv, lambda o=other: dev(x, zh, c, y, o))
         send(
@@ -526,11 +529,19 @@
         for r in range(2):
             mid_out[2 * r + s, 0] = mrecv[s, r].astype(BF16)
 
-    for pred, make in pending:
-
-        @pl.when(pred)
-        def _(make=make):
-            make().wait_send()
+    def wait_all(entries):
+        for pred, makers in entries:
+
+            @pl.when(pred)
+            def _(makers=makers):
+                for make in makers:
+                    make().wait_send()
+
+    for outer, entries in pending.values():
+        if outer is None:
+            wait_all(entries)
+        else:
+            pl.when(outer)(lambda entries=entries: wait_all(entries))
 
 
 def per_device(leaf, middle, root, s2, s1, o2, o1):

time: 216 us -> 216 us (level)
  no operation moved by 1% of the time
where the time goes in v7:
time: 216 us; the launch traced here: 215 us
  Pallas kernels  203 us (94%)
  local copies, waits for them, and re-layouts  11.5 us (5%)
    pallas_call x1, Pallas kernels, per_device(): pl.pallas_call(kernel, out_shape=outs, in_specs=[vmem] * 5 + [smem] * 2,...  203 us
    unnamed x9, local copies, waits for them, and re-layouts  11.5 us

profile of v7, /device:TPU:500, one launch (start us, length us, event | category | flops | bytes accessed | tf_op | source)
XLA Modules:
  0.0 215.2 jit_solution(11686158304119712904)
XLA Ops:
  0.6 0.0 copy-start
  0.6 2.0 copy.20
  2.7 2.3 %copy.19 = f32[4,256,1,256]{3,1,2,0:T(8,128)} copy(f32[4,256,1,256]{3,2,1,0:T(1,128)} %param.8) | data formatting | bytes 2097152
  4.9 0.0 copy-done
  4.9 1.6 copy.18
  6.5 203.0 %window.1 = (bf16[8,1,8,256]{3,2,1,0:T(8,128)(2,1)}, bf16[4,1,8,256]{3,2,1,0:T(8,128)(2,1)}, bf16[2,1,8,256]{3,2,1,0:T(8,128)(2,1)}, bf16[2,256,256]{2,1,0:T(8,128)(2,1)}) custom-call(f32[8,256,256]{2,1,0:T(8,128)} %bitcast.12, f32[4,256,256]{2,1,0:T(8,128)} %bitcast.13, f32[2,256,256]{2,1,0:T(8,128)} %bitcast.14, s32[4,32,256]{2,1,0:T(8,128)} %s2_.1, ...), custom_call_target="tpu_custom_call" | custom-call | tf_op jit(solution)/shard_map/window/pallas_call | solution.py:585
  209.6 1.4 copy.25
  210.9 1.3 copy.26
  212.3 1.3 copy.27
  213.6 1.7 copy.28
Async XLA Ops:
  0.6 4.3 %copy-start = (f32[8,256,1,256]{3,2,1,0:T(1,128)S(1)}, f32[8,256,1,256]{3,2,1,0:T(1,128)}, u32[]{:S(2)}) copy-start(f32[8,256,1,256]{3,2,1,0:T(1,128)} %param.7) | copy-start | bytes 6291460
